TPU v7x, 256 devices: a whole 4x4x8 slice. The times are simulated.
256 devices in a mesh: gx: 16 (over x, z_hi), gy: 8 (over z_lo, y), gz: 2 (over core).
Axes of the slice: x: 4, y: 4, z: 8 (z_hi: 4, z_lo: 2; z = z_hi * 2 + z_lo), core: 2. Of those that a mesh axis runs over, the one named last changes fastest.
Arguments:
- state: float32 [5, 128, 128, 256], P(None, 'gx', 'gy', 'gz'), may hold values from -2 to 10, as said below
- adjoint: float32 [5, 128, 128, 256], P(None, 'gx', 'gy', 'gz'), may hold values from -6 to 6
- metric: float32 [9, 128, 128, 256], P(None, 'gx', 'gy', 'gz'), may hold values from -0.6 to 2.5, as said below
- jacobian: float32 [128, 128, 256], P('gx', 'gy', 'gz'), may hold values from 0.5 to 2
- boundary_kind_code: int32 [32, 32, 64], P('gx', 'gy', 'gz'), may hold values from 0 to 1
- orient: int32 [3, 32, 32, 64], P(None, 'gx', 'gy', 'gz'), may hold values from 0 to 1
Outputs:
- adjoint_residual: float32 [5, 128, 128, 256], P(None, 'gx', 'gy', 'gz')
Inputs may be any that keep to these rules, and one draw needn't show every extreme that they name: `state`: conserved variables of a gas with positive density and positive pressure. `metric`: in each direction's vector, the component along that direction is positive. `boundary_kind_code`: 0 marks a wall, 1 a farfield; read only on faces of the domain's boundary. `orient`: 1 reverses the facing of the first tangential index across the element's upper face; ignored on the domain's upper boundary.
All inputs are finite; a program needn't handle non-finite values.
Results may differ from a plain program's by a relative error of at most 0.0003.
Values sent between devices are 32-bit elements; how exact they have to be, the bound alone decides.
A program may use at most 192 MiB of HBM per device.

v0:
```python
import jax
import jax.numpy as jnp
import numpy as np
from jax import lax
from jax.experimental import pallas as pl
from jax.experimental.pallas import tpu as pltpu
from jax.sharding import PartitionSpec as P

INFLOW_STATE = (1.0, 0.4, 0.0, 0.1, 2.085)
MESH = pl.DeviceIdType.MESH
SLOTS = 7


def lobatto_matrix():
    points = np.array([-1.0, -1.0 / np.sqrt(5.0), 1.0 / np.sqrt(5.0), 1.0])
    weights = np.array(
        [
            1.0 / np.prod([points[place] - points[other] for other in range(4) if other != place])
            for place in range(4)
        ]
    )
    table = np.zeros((4, 4))
    for place in range(4):
        for other in range(4):
            if other != place:
                table[place, other] = (
                    weights[other] / weights[place] / (points[place] - points[other])
                )
        table[place, place] = -np.sum(table[place])
    return table


QUAD = (1.0, 5.0, 5.0, 1.0)
TABLE = lobatto_matrix()


def rcp(value):
    guess = pl.reciprocal(value, approx=True)
    return guess * (2.0 - value * guess)


def dot3(first, second):
    return first[0] * second[0] + first[1] * second[1] + first[2] * second[2]


def log_terms(a, b, log_a, log_b, inv_a, inv_b):
    s = a + b
    rs = rcp(s)
    f = (a - b) * rs
    q = f * f
    small = q < 0.01
    series = 1.0 + q * (1.0 / 3.0 + q * (1.0 / 5.0 + q * (1.0 / 7.0)))
    slope = f * (2.0 / 3.0 + q * (4.0 / 5.0 + q * (6.0 / 7.0)))
    rf = rcp(f)
    logged = (log_a - log_b) * rf
    log_slope = ((s * inv_a) * (s * inv_b) - logged) * rf
    return s, rs, f, jnp.where(small, series, logged), jnp.where(small, slope, log_slope)


def pair(left, right, scale, left_weight=1.0, right_weight=1.0, face=False):
    rho_l, vl, beta_l = left[0], left[1:4], left[4]
    rho_r, vr, beta_r = right[0], right[1:4], right[4]
    wl, wr = left[9:14], right[9:14]
    if left_weight != 1.0:
        wl = [left_weight * w for w in wl]
    if right_weight != 1.0:
        wr = [right_weight * w for w in wr]
    om = [x - y for x, y in zip(wl, wr)]
    o0, ov, oh = om[0], om[1:4], om[4]
    g = [(x + y) * scale for x, y in zip(left[14:17], right[14:17])]
    vs = [x + y for x, y in zip(vl, vr)]
    rho_s, _, rho_f, rho_factor, rho_slope = log_terms(
        rho_l, rho_r, left[5], right[5], left[7], right[7]
    )
    _, beta_i, beta_f, beta_factor, beta_slope = log_terms(
        beta_l, beta_r, left[6], right[6], left[8], right[8]
    )
    p = rcp(rho_factor)
    half_p = 0.5 * p
    mean = rho_s * half_p
    through = dot3(vs, g)
    a = o0 + 0.5 * dot3(ov, vs) + oh * (dot3(vl, vr) + 5.0 * (beta_factor * beta_i))
    b = dot3(ov, g) + oh * through
    ph = rho_s * beta_i
    bi = beta_i * b
    ua = through * a
    k = half_p * (p * rho_slope)
    x = ua * (half_p + k * rho_f) + bi
    y = ua * k
    d_rho_l, d_rho_r = x - y, x + y
    t = mean * through
    e = t * oh
    c = mean * a + ph * oh
    half_t = 0.5 * t
    z = [c * gg + half_t * oo for gg, oo in zip(g, ov)]
    d_v_l = [zz + e * v for zz, v in zip(z, vr)]
    d_v_r = [zz + e * v for zz, v in zip(z, vl)]
    e5 = (-5.0 * e) * (beta_i * beta_i)
    x = e5 * (beta_factor + beta_slope * beta_f) - ph * bi
    y = e5 * beta_slope
    d_beta_l, d_beta_r = x - y, x + y
    if face:
        xl = o0 + dot3(ov, vl) + oh * (10.0 * left[8] * 0.5 + dot3(vl, vl))
        xr = o0 + dot3(ov, vr) + oh * (10.0 * right[8] * 0.5 + dot3(vr, vr))
        kappa = rho_l * xl - rho_r * xr
        n2 = dot3(g, g)
        half_len = 0.5 * jnp.sqrt(n2)
        cl = jnp.sqrt(1.4 * left[8])
        cr = jnp.sqrt(1.4 * right[8])
        sl = dot3(vl, g)
        sr = dot3(vr, g)
        mean_square = 0.5 * (sl * sl + sr * sr)
        rt = lax.rsqrt(mean_square)
        sigma = mean_square * rt + half_len * (cl + cr)
        kr = (0.5 * kappa) * rt
        krl, krr = kr * sl, kr * sr
        ml, mr = sigma * rho_l, sigma * rho_r
        oh2 = 2.0 * oh
        el, er = ml * oh2, mr * oh2
        d_v_l = [d + krl * gg + ml * oo + el * v for d, gg, oo, v in zip(d_v_l, g, ov, vl)]
        d_v_r = [d + krr * gg - mr * oo - er * v for d, gg, oo, v in zip(d_v_r, g, ov, vr)]
        d_rho_l = d_rho_l + sigma * xl
        d_rho_r = d_rho_r - sigma * xr
        kl = kappa * half_len
        d_beta_l = d_beta_l - left[8] * (kl * cl + 5.0 * (el * left[8]))
        d_beta_r = d_beta_r - right[8] * (kl * cr - 5.0 * (er * right[8]))
    return [d_rho_l, *d_v_l, d_beta_l], [d_rho_r, *d_v_r, d_beta_r]


def node_extras(rho, beta, inv_rho, inv_beta):
    return [0.5 * jnp.log(rho), 0.5 * jnp.log(beta), inv_rho, inv_beta]


def line(load, store):
    total = [None] * 4
    for a in range(4):
        for b in range(a + 1, 4):
            factor = 2.0 * QUAD[a] * TABLE[a, b] / 4.0
            wa, wb = 1.0 / QUAD[a], 1.0 / QUAD[b]
            if wa == wb:
                factor, wa, wb = factor * wa, 1.0, 1.0
            first, second = pair(load(a), load(b), float(factor), wa, wb)
            for node, part in ((a, first), (b, second)):
                total[node] = part if total[node] is None else [x + y for x, y in zip(total[node], part)]
    for a in range(4):
        store(a, total[a])


def kernel(
    nx, ny,
    state_ref, adj_ref, met_ref, jac_ref, code_ref, orient_ref, out_ref,
    st, ad, mt, jc, cd, ori, nb, tb, acc, acct, send, recv, gout, mb, el,
    load_sem, send_sem, recv_sem,
):
    f32 = jnp.float32
    ix, iy, iz = lax.axis_index("gx"), lax.axis_index("gy"), lax.axis_index("gz")
    low_x, high_x, low_y, high_y = ix == 0, ix == nx - 1, iy == 0, iy == ny - 1
    ids = [
        {"gx": lax.max(ix - 1, 0)}, {"gx": lax.min(ix + 1, nx - 1)},
        {"gy": lax.max(iy - 1, 0)}, {"gy": lax.min(iy + 1, ny - 1)},
        {"gz": 1 - iz},
    ]
    edge = [low_x, high_x, low_y, high_y, None]
    spans = [(0, 2), (2, 2), (4, 1), (5, 1), (6, 1)]

    loads = [
        pltpu.make_async_copy(src, dst, load_sem.at[n])
        for n, (src, dst) in enumerate(
            ((code_ref, cd), (orient_ref, ori), (state_ref, st), (adj_ref, ad), (jac_ref, jc), (met_ref, mt))
        )
    ]
    for copy in loads:
        copy.start()

    barrier = pltpu.get_barrier_semaphore()
    for side in range(5):
        def greet(side=side):
            pl.semaphore_signal(barrier, inc=1, device_id=ids[side], device_id_type=MESH)

        if edge[side] is None:
            greet()
        else:
            pl.when(jnp.logical_not(edge[side]))(greet)

            @pl.when(edge[side])
            def _(side=side):
                first, count = spans[side]
                for slot in range(first, first + count):
                    for n in range(13):
                        recv[slot, n] = jnp.zeros((8, 128), f32)

    sub = lax.broadcasted_iota(jnp.int32, (8, 128), 0)
    lane = lax.broadcasted_iota(jnp.int32, (8, 128), 1)
    sub_flip = sub ^ 3
    lane_flip = lane ^ 48

    def flip_sub(value):
        return jnp.take_along_axis(value, sub_flip, axis=0, mode="promise_in_bounds")

    def flip_lane(value):
        return jnp.take_along_axis(value, lane_flip, axis=1, mode="promise_in_bounds")

    loads[0].wait()
    loads[1].wait()
    el[0:8, :] = cd[...].astype(f32)
    el[8:32, :] = ori[...].astype(f32)
    spread = (
        lax.broadcasted_iota(jnp.int32, (32, 128), 1) // 4 == lax.broadcasted_iota(jnp.int32, (32, 128), 0)
    ).astype(f32)
    wide = jnp.dot(el[...], spread, preferred_element_type=f32)
    xy = lax.broadcasted_iota(jnp.int32, (8, 128), 1)
    spread_xy = ((xy // 64) * 4 + (xy % 16) // 4 == sub).astype(f32)
    contract = (((0,), (0,)), ((), ()))
    code_z = lax.dot_general(el[0:8, :], spread_xy, contract, preferred_element_type=f32)
    flag_z = lax.dot_general(el[24:32, :], spread_xy, contract, preferred_element_type=f32)

    def two_rows(first, second):
        return jnp.where(
            sub < 4,
            jnp.broadcast_to(wide[first : first + 1], (8, 128)),
            jnp.broadcast_to(wide[second : second + 1], (8, 128)),
        )

    def x_rows(base, ex, half):
        return two_rows(base + ex * 4 + 2 * half, base + ex * 4 + 2 * half + 1)

    def y_rows(base, ey):
        return two_rows(base + ey, base + 4 + ey)

    codes = [x_rows(0, 0, 0), x_rows(0, 0, 1), x_rows(0, 1, 0), x_rows(0, 1, 1), y_rows(0, 0), y_rows(0, 3)]
    low_row = sub % 2 == 0
    codes.append(
        jnp.where(
            low_row,
            jnp.broadcast_to(code_z[0:1], (8, 128)),
            jnp.broadcast_to(code_z[31:32], (8, 128)),
        )
    )
    one, zero = jnp.ones((8, 128), f32), jnp.zeros((8, 128), f32)
    at_edge = [jnp.where(e, one, zero) for e in (low_x, low_x, high_x, high_x, low_y, high_y)]
    at_edge.append(jnp.where(low_row, jnp.where(iz == 0, one, zero), jnp.where(iz == 1, one, zero)))
    signs = [-1.5 * one, -1.5 * one, 1.5 * one, 1.5 * one, -1.5 * one, 1.5 * one, jnp.where(low_row, -1.5 * one, 1.5 * one)]
    for slot in range(SLOTS):
        mb[slot, 0] = signs[slot]
        far = at_edge[slot] * codes[slot]
        mb[slot, 1] = far
        mb[slot, 2] = at_edge[slot] - far
    flag_x_mid = [x_rows(8, 0, half) > 0.5 for half in range(2)]
    flag_x_top = [(x_rows(8, 1, half) > 0.5) & jnp.logical_not(high_x) for half in range(2)]
    flag_y_mid = [y_rows(16, ey) > 0.5 for ey in range(3)]
    flag_y_top = (y_rows(16, 3) > 0.5) & jnp.logical_not(high_y)
    flag_z_top = (jnp.broadcast_to(flag_z[31:32], (8, 128)) > 0.5) & jnp.logical_not(low_row) & (iz == 0)

    def convert(rows):
        rho, m, energy = st[0, rows], [st[n, rows] for n in (1, 2, 3)], st[4, rows]
        r = rcp(rho)
        v = [x * r for x in m]
        pressure = 0.4 * (energy - 0.5 * dot3(m, v))
        beta = (0.5 * rho) * rcp(pressure)
        rj = -rcp(jc[rows])
        w = [ad[n, rows] * rj for n in range(5)]
        w[4] = 0.5 * w[4]
        values = [rho, *v, beta, *node_extras(rho, beta, 0.5 * r, pressure * r), *w]
        for n, value in enumerate(values):
            nb[n, rows] = value
        return values

    for load in loads[2:]:
        load.wait()

    def pack(slot, values, flag=None, flip=None):
        for n, value in enumerate(values):
            if flag is not None:
                value = jnp.where(flag, flip(value), value)
            send[slot, n] = value

    for slot, block in ((0, 0), (1, 1), (2, 14), (3, 15)):
        rows = pl.ds(block * 8, 8)
        values = convert(rows)
        raw = values[0:5] + values[9:14] + [mt[n, rows] for n in range(3)]
        if slot < 2:
            pack(slot, raw)
        else:
            pack(slot, raw, flag_x_top[slot - 2], flip_sub)

    waits = lax.convert_element_type(
        5 - jnp.where(low_x, 1, 0) - jnp.where(high_x, 1, 0) - jnp.where(low_y, 1, 0) - jnp.where(high_y, 1, 0), jnp.int32
    )
    pl.semaphore_wait(barrier, waits)

    landing = [1, 0, 3, 2, 4]
    copies = []
    for side in range(5):
        first, count = spans[side]
        target, _ = spans[landing[side]]
        copies.append(
            pltpu.make_async_remote_copy(
                src_ref=send.at[pl.ds(first, count)],
                dst_ref=recv.at[pl.ds(target, count)],
                send_sem=send_sem.at[side],
                recv_sem=recv_sem.at[landing[side]],
                device_id=ids[side],
                device_id_type=MESH,
            )
        )

    def on_side(side, act):
        if edge[side] is None:
            act()
        else:
            pl.when(jnp.logical_not(edge[side]))(act)

    on_side(0, lambda: copies[0].start())
    on_side(1, lambda: copies[1].start())

    @pl.loop(2, 14)
    def _(block):
        convert(pl.ds(pl.multiple_of(block * 8, 8), 8))

    def load_y(y):
        rows = pl.ds(y, 8, stride=16)
        return [nb[n, rows] for n in range(14)] + [mt[3 + n, rows] for n in range(3)]

    for slot, y in ((4, 0), (5, 15)):
        values = load_y(y)
        raw = values[0:5] + values[9:17]
        if slot == 4:
            pack(slot, raw)
        else:
            pack(slot, raw, flag_y_top, flip_sub)
    on_side(2, lambda: copies[2].start())
    on_side(3, lambda: copies[3].start())

    for n in range(5):
        tb[n, 0:128] = jnp.transpose(nb[n])
        tb[9 + n, 0:128] = jnp.transpose(nb[9 + n])
    for n in range(3):
        tb[14 + n, 0:128] = jnp.transpose(mt[6 + n])
    raw_t = [0, 1, 2, 3, 4, 9, 10, 11, 12, 13, 14, 15, 16]
    low_z = [jnp.broadcast_to(tb[n, 0:1], (8, 128)) for n in raw_t]
    high_z = [jnp.broadcast_to(tb[n, 127:128], (8, 128)) for n in raw_t]
    pack(6, [jnp.where(low_row, x, y) for x, y in zip(low_z, high_z)], flag_z_top, flip_lane)
    copies[4].start()

    @pl.loop(0, 16)
    def _(block):
        rows = pl.ds(pl.multiple_of(block * 8, 8), 8)
        rho, beta = tb[0, rows], tb[4, rows]
        for n, value in enumerate(node_extras(rho, beta, 0.5 * rcp(rho), 0.5 * rcp(beta))):
            tb[5 + n, rows] = value

    def load_x(rows):
        return [nb[n, rows] for n in range(14)] + [mt[n, rows] for n in range(3)]

    @pl.loop(0, 4)
    def _(chunk):
        base = (chunk // 2) * 64 + (chunk % 2) * 8

        def at(a):
            return pl.ds(pl.multiple_of(base + a * 16, 8), 8)

        def store(a, total):
            for n in range(5):
                acc[n, at(a)] = total[n]

        line(lambda a: load_x(at(a)), store)

    def add(ref, rows, parts):
        for n in range(5):
            ref[n, rows] = ref[n, rows] + parts[n]

    def flipped(values, flag, flip):
        return [jnp.where(flag, flip(value), value) for value in values]

    for half in range(2):
        lower, upper = pl.ds(48 + 8 * half, 8), pl.ds(64 + 8 * half, 8)
        left = flipped(load_x(lower), flag_x_mid[half], flip_sub)
        to_l, to_u = pair(left, load_x(upper), 1.5, face=True)
        add(acc, lower, flipped(to_l, flag_x_mid[half], flip_sub))
        add(acc, upper, to_u)

    @pl.loop(0, 4)
    def _(chunk):
        def store(a, total):
            add(acc, pl.ds(chunk * 4 + a, 8, stride=16), total)

        line(lambda a: load_y(chunk * 4 + a), store)

    for ey in range(3):
        left = flipped(load_y(4 * ey + 3), flag_y_mid[ey], flip_sub)
        to_l, to_u = pair(left, load_y(4 * ey + 4), 1.5, face=True)
        add(acc, pl.ds(4 * ey + 3, 8, stride=16), flipped(to_l, flag_y_mid[ey], flip_sub))
        add(acc, pl.ds(4 * ey + 4, 8, stride=16), to_u)

    def rows_z(chunk, a):
        return pl.ds(chunk * 32 + a, 8, stride=4)

    def load_z(rows):
        return [tb[n, rows] for n in range(17)]

    @pl.loop(0, 4)
    def _(chunk):
        def store(a, total):
            for n in range(5):
                acct[n, rows_z(chunk, a)] = total[n]

        line(lambda a: load_z(rows_z(chunk, a)), store)

    for chunk in range(4):
        flag = flag_z[8 * chunk : 8 * chunk + 8] > 0.5
        lower = rows_z(chunk, 3)
        left = flipped(load_z(lower), flag, flip_lane)
        upper = rows_z(chunk, 4)
        right = load_z(upper)
        to_l, to_u = pair(left, right, 1.5, face=True)
        to_l = flipped(to_l, flag, flip_lane)
        if chunk == 3:
            inside = sub < 7
            to_l = [jnp.where(inside, x, 0.0) for x in to_l]
            to_u = [jnp.where(inside, x, 0.0) for x in to_u]
        add(acct, lower, to_l)
        add(acct, upper, to_u)

    for side in (4, 2, 3, 0, 1):
        on_side(side, lambda side=side: copies[landing[side]].wait_recv())
    for n in range(13):
        recv[6, n] = pltpu.roll(recv[6, n], 1, 0)

    inflow = np.array(INFLOW_STATE)
    inflow_v = inflow[1:4] / inflow[0]
    inflow_p = 0.4 * (inflow[4] - 0.5 * np.sum(inflow[1:4] * inflow_v))
    far_values = [float(inflow[0]), *[float(x) for x in inflow_v], float(inflow[0] / (2.0 * inflow_p))]

    @pl.loop(0, SLOTS)
    def _(slot):
        own = [send[slot, n] for n in range(13)]
        other = [recv[slot, n] for n in range(13)]
        scale, far, wall = mb[slot, 0], mb[slot, 1], mb[slot, 2]
        is_far, is_wall = far > 0.5, wall > 0.5
        outside = is_far | is_wall
        g = own[10:13]
        turn = 2.0 * rcp(dot3(g, g))

        def mirror(v):
            along = turn * dot3(v, g)
            return [x - along * y for x, y in zip(v, g)]

        image = [own[0], *mirror(own[1:4]), own[4]]
        oth = [
            jnp.where(is_far, f, jnp.where(is_wall, i, o)) for f, i, o in zip(far_values, image, other[0:5])
        ]
        oth_w = [jnp.where(outside, 0.0, o) for o in other[5:10]]
        oth_g = [jnp.where(outside, i, o) for i, o in zip(g, other[10:13])]

        def full(prim, w, normal):
            return [*prim, *node_extras(prim[0], prim[4], 0.5 * rcp(prim[0]), 0.5 * rcp(prim[4])), *w, *normal]

        mine, theirs = pair(full(own[0:5], own[5:10], g), full(oth, oth_w, oth_g), scale, face=True)
        back = [theirs[0], *mirror(theirs[1:4]), theirs[4]]
        for n in range(5):
            gout[slot, n] = mine[n] + jnp.where(is_wall, back[n], 0.0)

    for slot, block in ((0, 0), (1, 1), (2, 14), (3, 15)):
        parts = [gout[slot, n] for n in range(5)]
        if slot >= 2:
            parts = flipped(parts, flag_x_top[slot - 2], flip_sub)
        add(acc, pl.ds(block * 8, 8), parts)
    add(acc, pl.ds(0, 8, stride=16), [gout[4, n] for n in range(5)])
    add(acc, pl.ds(15, 8, stride=16), flipped([gout[5, n] for n in range(5)], flag_y_top, flip_sub))
    for n in range(5):
        part = gout[6, n]
        part = jnp.where(flag_z_top, flip_lane(part), part)
        acct[n, 0:1] = acct[n, 0:1] + part[0:1]
        acct[n, 127:128] = acct[n, 127:128] + part[1:2]

    for n in range(5):
        acc[n] = acc[n] + jnp.transpose(acct[n, 0:128])

    @pl.loop(0, 16)
    def _(block):
        rows = pl.ds(pl.multiple_of(block * 8, 8), 8)
        v, beta, r = [nb[n, rows] for n in (1, 2, 3)], nb[4, rows], 2.0 * nb[7, rows]
        d_rho, d_v, d_beta = acc[0, rows], [acc[n, rows] for n in (1, 2, 3)], acc[4, rows]
        db = d_beta * (beta * r)
        d_p = (-0.8 * beta) * db
        out_ref[4, rows] = d_p
        for n in range(3):
            out_ref[1 + n, rows] = d_v[n] * r - d_p * v[n]
        out_ref[0, rows] = d_rho + db - r * dot3(d_v, v) + 0.5 * d_p * dot3(v, v)

    for side in (4, 2, 3, 0, 1):
        on_side(side, lambda side=side: copies[side].wait_send())


def solution(mesh):
    nx, ny, nz = mesh.shape["gx"], mesh.shape["gy"], mesh.shape["gz"]
    assert nz == 2

    def body(state, adjoint, metric, jacobian, boundary_kind_code, orient):
        assert state.shape == (5, 8, 16, 128)
        f32 = jnp.float32
        hbm = pl.BlockSpec(memory_space=pl.ANY)
        vmem = pltpu.VMEM
        out = pl.pallas_call(
            lambda *refs: kernel(nx, ny, *refs),
            out_shape=jax.ShapeDtypeStruct((5, 128, 128), f32),
            in_specs=[hbm] * 6,
            out_specs=pl.BlockSpec(memory_space=vmem),
            scratch_shapes=[
                vmem((5, 128, 128), f32),
                vmem((5, 128, 128), f32),
                vmem((9, 128, 128), f32),
                vmem((128, 128), f32),
                vmem((8, 32), jnp.int32),
                vmem((24, 32), jnp.int32),
                vmem((14, 128, 128), f32),
                vmem((17, 136, 128), f32),
                vmem((5, 128, 128), f32),
                vmem((5, 136, 128), f32),
                vmem((SLOTS, 13, 8, 128), f32),
                vmem((SLOTS, 13, 8, 128), f32),
                vmem((SLOTS, 5, 8, 128), f32),
                vmem((SLOTS, 3, 8, 128), f32),
                vmem((32, 32), f32),
                pltpu.SemaphoreType.DMA((6,)),
                pltpu.SemaphoreType.DMA((5,)),
                pltpu.SemaphoreType.DMA((5,)),
            ],
            compiler_params=pltpu.CompilerParams(
                collective_id=0, has_side_effects=True, vmem_limit_bytes=32 * 1024 * 1024
            ),
            name="adjoint_residual",
        )(
            state.reshape(5, 128, 128),
            adjoint.reshape(5, 128, 128),
            metric.reshape(9, 128, 128),
            jacobian.reshape(128, 128),
            boundary_kind_code.reshape(8, 32),
            orient.reshape(24, 32),
        )
        return out.reshape(5, 8, 16, 128)

    return jax.shard_map(
        body,
        mesh=mesh,
        in_specs=(
            P(None, "gx", "gy", "gz"),
            P(None, "gx", "gy", "gz"),
            P(None, "gx", "gy", "gz"),
            P("gx", "gy", "gz"),
            P("gx", "gy", "gz"),
            P(None, "gx", "gy", "gz"),
        ),
        out_specs=P(None, "gx", "gy", "gz"),
        check_vma=False,
    )
```

profile of v0, /device:TPU:36, one launch (start us, length us, event | category | flops | bytes accessed | tf_op | source)
XLA Modules:
  0.0 22.4 jit_solution(5769101445223499210)
XLA Ops:
  0.0 0.0 copy-start.5
  0.0 0.7 %copy-done.5 = s32[2,4,32]{2,1,0:T(4,128)S(1)} copy-done((s32[2,4,32]{2,1,0:T(4,128)S(1)}, s32[2,4,32]{2,1,0:T(4,128)}, u32[]{:S(2)}) %copy-start.5) | copy-done | bytes 1048
  0.7 0.0 copy-start
  0.7 1.1 %copy-done = f32[9,8,16,128]{3,2,1,0:T(8,128)S(1)} copy-done((f32[9,8,16,128]{3,2,1,0:T(8,128)S(1)}, f32[9,8,16,128]{3,2,1,0:T(8,128)}, u32[]{:S(2)}) %copy-start) | copy-done | bytes 589848
  1.8 0.0 copy-start.1
  1.8 1.0 %copy-done.1 = f32[5,8,16,128]{3,2,1,0:T(8,128)S(1)} copy-done((f32[5,8,16,128]{3,2,1,0:T(8,128)S(1)}, f32[5,8,16,128]{3,2,1,0:T(8,128)}, u32[]{:S(2)}) %copy-start.1) | copy-done | bytes 327704
  2.7 0.0 copy-start.2
  2.7 1.0 %copy-done.2 = f32[5,8,16,128]{3,2,1,0:T(8,128)S(1)} copy-done((f32[5,8,16,128]{3,2,1,0:T(8,128)S(1)}, f32[5,8,16,128]{3,2,1,0:T(8,128)}, u32[]{:S(2)}) %copy-start.2) | copy-done | bytes 327704
  3.7 0.0 copy-start.3
  3.7 0.8 %copy-done.3 = f32[8,16,128]{2,1,0:T(8,128)S(1)} copy-done((f32[8,16,128]{2,1,0:T(8,128)S(1)}, f32[8,16,128]{2,1,0:T(8,128)}, u32[]{:S(2)}) %copy-start.3) | copy-done | bytes 65560
  4.5 0.0 copy-start.4
  4.5 0.7 %copy-done.4 = s32[3,2,4,32]{3,2,1,0:T(4,128)S(1)} copy-done((s32[3,2,4,32]{3,2,1,0:T(4,128)S(1)}, s32[3,2,4,32]{3,2,1,0:T(4,128)}, u32[]{:S(2)}) %copy-start.4) | copy-done | bytes 3096
  5.2 16.4 %adjoint_residual.1 = f32[5,128,128]{2,1,0:T(8,128)S(1)} custom-call(f32[5,128,128]{2,1,0:T(8,128)S(1)} %bitcast.9, f32[5,128,128]{2,1,0:T(8,128)S(1)} %bitcast.10, f32[9,128,128]{2,1,0:T(8,128)S(1)} %bitcast.8, f32[128,128]{1,0:T(8,128)S(1)} %bitcast.11, s32[8,32]{1,0:T(8,128)S(1)} %bitcast.13, s32[24,32]{1,0:T(8,128)S(1)} %bitcast.12), custom_call_target="tpu_custom_call" | custom-call | tf_op jit(solution)/shard_map/adjoint_residual/pallas_call | solution.py:504
  21.7 0.7 %copy.8 = f32[5,8,16,128]{3,2,1,0:T(8,128)} copy(f32[5,8,16,128]{3,2,1,0:T(8,128)S(1)} %bitcast.7) | data formatting | bytes 655360
Async XLA Ops:
  0.0 0.7 %copy-start.5 = (s32[2,4,32]{2,1,0:T(4,128)S(1)}, s32[2,4,32]{2,1,0:T(4,128)}, u32[]{:S(2)}) copy-start(s32[2,4,32]{2,1,0:T(4,128)} %param.10) | copy-start | bytes 3076
  0.7 1.1 %copy-start = (f32[9,8,16,128]{3,2,1,0:T(8,128)S(1)}, f32[9,8,16,128]{3,2,1,0:T(8,128)}, u32[]{:S(2)}) copy-start(f32[9,8,16,128]{3,2,1,0:T(8,128)} %param.8) | copy-start | bytes 1769476
  1.8 1.0 %copy-start.1 = (f32[5,8,16,128]{3,2,1,0:T(8,128)S(1)}, f32[5,8,16,128]{3,2,1,0:T(8,128)}, u32[]{:S(2)}) copy-start(f32[5,8,16,128]{3,2,1,0:T(8,128)} %param.6) | copy-start | bytes 983044
  2.7 1.0 %copy-start.2 = (f32[5,8,16,128]{3,2,1,0:T(8,128)S(1)}, f32[5,8,16,128]{3,2,1,0:T(8,128)}, u32[]{:S(2)}) copy-start(f32[5,8,16,128]{3,2,1,0:T(8,128)} %param.7) | copy-start | bytes 983044
  3.7 0.8 %copy-start.3 = (f32[8,16,128]{2,1,0:T(8,128)S(1)}, f32[8,16,128]{2,1,0:T(8,128)}, u32[]{:S(2)}) copy-start(f32[8,16,128]{2,1,0:T(8,128)} %param.9) | copy-start | bytes 196612
  4.5 0.7 %copy-start.4 = (s32[3,2,4,32]{3,2,1,0:T(4,128)S(1)}, s32[3,2,4,32]{3,2,1,0:T(4,128)}, u32[]{:S(2)}) copy-start(s32[3,2,4,32]{3,2,1,0:T(4,128)} %param.11) | copy-start | bytes 9220
where the time goes:
time: 22.7 us; the launch traced here: 22.4 us
  Pallas kernels  16.4 us (72%)
  local copies, waits for them, and re-layouts  5.97 us (26%)
    pallas_call x1, Pallas kernels, body(): pl.pallas_call(lambda *refs: kernel(nx, ny, *refs), out_shape=jax.ShapeDt...  16.4 us
    unnamed x13, local copies, waits for them, and re-layouts  5.97 us

commit v1 on v0

--- a/solution.py
+++ b/solution.py
@@ -163,15 +163,16 @@
     edge = [low_x, high_x, low_y, high_y, None]
     spans = [(0, 2), (2, 2), (4, 1), (5, 1), (6, 1)]
 
-    loads = [
-        pltpu.make_async_copy(src, dst, load_sem.at[n])
-        for n, (src, dst) in enumerate(
-            ((code_ref, cd), (orient_ref, ori), (state_ref, st), (adj_ref, ad), (jac_ref, jc), (met_ref, mt))
-        )
-    ]
-    for copy in loads:
-        copy.start()
-
+    outer = [pl.ds(0, 16), pl.ds(112, 16)]
+    inner = pl.ds(16, 96)
+    moves = [(code_ref, cd), (orient_ref, ori)]
+    for rows in outer:
+        moves += [(src.at[:, rows], dst.at[:, rows]) for src, dst in ((state_ref, st), (adj_ref, ad))]
+        moves += [(jac_ref.at[rows], jc.at[rows]), (met_ref.at[0:3, rows], mt.at[0:3, rows])]
+    moves += [(src.at[:, inner], dst.at[:, inner]) for src, dst in ((state_ref, st), (adj_ref, ad))]
+    moves += [(jac_ref.at[inner], jc.at[inner]), (met_ref.at[3:9], mt.at[3:9])]
+    moves.append((met_ref.at[0:3, inner], mt.at[0:3, inner]))
+    loads = [pltpu.make_async_copy(src, dst, load_sem.at[n]) for n, (src, dst) in enumerate(moves)]
     barrier = pltpu.get_barrier_semaphore()
     for side in range(5):
         def greet(side=side):
@@ -181,7 +182,10 @@
             greet()
         else:
             pl.when(jnp.logical_not(edge[side]))(greet)
-
+    for copy in loads:
+        copy.start()
+    for side in range(4):
+        if edge[side] is not None:
             @pl.when(edge[side])
             def _(side=side):
                 first, count = spans[side]
@@ -265,7 +269,7 @@
             nb[n, rows] = value
         return values
 
-    for load in loads[2:]:
+    for load in loads[2:10]:
         load.wait()
 
     def pack(slot, values, flag=None, flip=None):
@@ -289,20 +293,18 @@
     pl.semaphore_wait(barrier, waits)
 
     landing = [1, 0, 3, 2, 4]
-    copies = []
-    for side in range(5):
-        first, count = spans[side]
-        target, _ = spans[landing[side]]
-        copies.append(
-            pltpu.make_async_remote_copy(
-                src_ref=send.at[pl.ds(first, count)],
-                dst_ref=recv.at[pl.ds(target, count)],
-                send_sem=send_sem.at[side],
-                recv_sem=recv_sem.at[landing[side]],
-                device_id=ids[side],
-                device_id_type=MESH,
-            )
+    def copy_of(side, place):
+        source, target = spans[side][0] + place, spans[landing[side]][0] + place
+        return pltpu.make_async_remote_copy(
+            src_ref=send.at[source],
+            dst_ref=recv.at[target],
+            send_sem=send_sem.at[source],
+            recv_sem=recv_sem.at[target],
+            device_id=ids[side],
+            device_id_type=MESH,
         )
+
+    copies = [[copy_of(side, place) for place in range(spans[side][1])] for side in range(5)]
 
     def on_side(side, act):
         if edge[side] is None:
@@ -310,12 +312,18 @@
         else:
             pl.when(jnp.logical_not(edge[side]))(act)
 
-    on_side(0, lambda: copies[0].start())
-    on_side(1, lambda: copies[1].start())
+    for place in range(2):
+        for side in (0, 1):
+            on_side(side, copies[side][place].start)
+
+    for load in loads[10:13]:
+        load.wait()
 
     @pl.loop(2, 14)
     def _(block):
         convert(pl.ds(pl.multiple_of(block * 8, 8), 8))
+
+    loads[13].wait()
 
     def load_y(y):
         rows = pl.ds(y, 8, stride=16)
@@ -328,8 +336,8 @@
             pack(slot, raw)
         else:
             pack(slot, raw, flag_y_top, flip_sub)
-    on_side(2, lambda: copies[2].start())
-    on_side(3, lambda: copies[3].start())
+    on_side(2, copies[2][0].start)
+    on_side(3, copies[3][0].start)
 
     for n in range(5):
         tb[n, 0:128] = jnp.transpose(nb[n])
@@ -340,7 +348,7 @@
     low_z = [jnp.broadcast_to(tb[n, 0:1], (8, 128)) for n in raw_t]
     high_z = [jnp.broadcast_to(tb[n, 127:128], (8, 128)) for n in raw_t]
     pack(6, [jnp.where(low_row, x, y) for x, y in zip(low_z, high_z)], flag_z_top, flip_lane)
-    copies[4].start()
+    copies[4][0].start()
 
     @pl.loop(0, 16)
     def _(block):
@@ -348,6 +356,8 @@
         rho, beta = tb[0, rows], tb[4, rows]
         for n, value in enumerate(node_extras(rho, beta, 0.5 * rcp(rho), 0.5 * rcp(beta))):
             tb[5 + n, rows] = value
+
+    loads[14].wait()
 
     def load_x(rows):
         return [nb[n, rows] for n in range(14)] + [mt[n, rows] for n in range(3)]
@@ -421,8 +431,8 @@
         add(acct, lower, to_l)
         add(acct, upper, to_u)
 
-    for side in (4, 2, 3, 0, 1):
-        on_side(side, lambda side=side: copies[landing[side]].wait_recv())
+    for side in (4, 2, 3):
+        on_side(side, copies[landing[side]][0].wait_recv)
     for n in range(13):
         recv[6, n] = pltpu.roll(recv[6, n], 1, 0)
 
@@ -431,8 +441,7 @@
     inflow_p = 0.4 * (inflow[4] - 0.5 * np.sum(inflow[1:4] * inflow_v))
     far_values = [float(inflow[0]), *[float(x) for x in inflow_v], float(inflow[0] / (2.0 * inflow_p))]
 
-    @pl.loop(0, SLOTS)
-    def _(slot):
+    def side_faces(slot):
         own = [send[slot, n] for n in range(13)]
         other = [recv[slot, n] for n in range(13)]
         scale, far, wall = mb[slot, 0], mb[slot, 1], mb[slot, 2]
@@ -457,18 +466,17 @@
 
         mine, theirs = pair(full(own[0:5], own[5:10], g), full(oth, oth_w, oth_g), scale, face=True)
         back = [theirs[0], *mirror(theirs[1:4]), theirs[4]]
-        for n in range(5):
-            gout[slot, n] = mine[n] + jnp.where(is_wall, back[n], 0.0)
-
-    for slot, block in ((0, 0), (1, 1), (2, 14), (3, 15)):
-        parts = [gout[slot, n] for n in range(5)]
-        if slot >= 2:
-            parts = flipped(parts, flag_x_top[slot - 2], flip_sub)
-        add(acc, pl.ds(block * 8, 8), parts)
-    add(acc, pl.ds(0, 8, stride=16), [gout[4, n] for n in range(5)])
-    add(acc, pl.ds(15, 8, stride=16), flipped([gout[5, n] for n in range(5)], flag_y_top, flip_sub))
+        return [x + jnp.where(is_wall, y, 0.0) for x, y in zip(mine, back)]
+
+    @pl.loop(4, SLOTS)
+    def _(slot):
+        for n, part in enumerate(side_faces(slot)):
+            gout[slot - 4, n] = part
+
+    add(acc, pl.ds(0, 8, stride=16), [gout[0, n] for n in range(5)])
+    add(acc, pl.ds(15, 8, stride=16), flipped([gout[1, n] for n in range(5)], flag_y_top, flip_sub))
     for n in range(5):
-        part = gout[6, n]
+        part = gout[2, n]
         part = jnp.where(flag_z_top, flip_lane(part), part)
         acct[n, 0:1] = acct[n, 0:1] + part[0:1]
         acct[n, 127:128] = acct[n, 127:128] + part[1:2]
@@ -476,11 +484,9 @@
     for n in range(5):
         acc[n] = acc[n] + jnp.transpose(acct[n, 0:128])
 
-    @pl.loop(0, 16)
-    def _(block):
-        rows = pl.ds(pl.multiple_of(block * 8, 8), 8)
+    def finish(rows, parts):
         v, beta, r = [nb[n, rows] for n in (1, 2, 3)], nb[4, rows], 2.0 * nb[7, rows]
-        d_rho, d_v, d_beta = acc[0, rows], [acc[n, rows] for n in (1, 2, 3)], acc[4, rows]
+        d_rho, d_v, d_beta = parts[0], parts[1:4], parts[4]
         db = d_beta * (beta * r)
         d_p = (-0.8 * beta) * db
         out_ref[4, rows] = d_p
@@ -488,8 +494,23 @@
             out_ref[1 + n, rows] = d_v[n] * r - d_p * v[n]
         out_ref[0, rows] = d_rho + db - r * dot3(d_v, v) + 0.5 * d_p * dot3(v, v)
 
+    @pl.loop(2, 14)
+    def _(block):
+        rows = pl.ds(pl.multiple_of(block * 8, 8), 8)
+        finish(rows, [acc[n, rows] for n in range(5)])
+
+    for slot in (0, 2, 1, 3):
+        on_side(slot // 2, copies[landing[slot // 2]][slot % 2].wait_recv)
+
+        rows = pl.ds((slot // 2) * 112 + (slot % 2) * 8, 8)
+        parts = side_faces(slot)
+        if slot >= 2:
+            parts = flipped(parts, flag_x_top[slot - 2], flip_sub)
+        finish(rows, [acc[n, rows] + part for n, part in enumerate(parts)])
+
     for side in (4, 2, 3, 0, 1):
-        on_side(side, lambda side=side: copies[side].wait_send())
+        for copy in copies[side]:
+            on_side(side, copy.wait_send)
 
 
 def solution(mesh):
@@ -499,7 +520,7 @@
     def body(state, adjoint, metric, jacobian, boundary_kind_code, orient):
         assert state.shape == (5, 8, 16, 128)
         f32 = jnp.float32
-        hbm = pl.BlockSpec(memory_space=pl.ANY)
+        hbm = pl.BlockSpec(memory_space=pltpu.HBM)
         vmem = pltpu.VMEM
         out = pl.pallas_call(
             lambda *refs: kernel(nx, ny, *refs),
@@ -519,24 +540,29 @@
                 vmem((5, 136, 128), f32),
                 vmem((SLOTS, 13, 8, 128), f32),
                 vmem((SLOTS, 13, 8, 128), f32),
-                vmem((SLOTS, 5, 8, 128), f32),
+                vmem((3, 5, 8, 128), f32),
                 vmem((SLOTS, 3, 8, 128), f32),
                 vmem((32, 32), f32),
-                pltpu.SemaphoreType.DMA((6,)),
-                pltpu.SemaphoreType.DMA((5,)),
-                pltpu.SemaphoreType.DMA((5,)),
+                pltpu.SemaphoreType.DMA((15,)),
+                pltpu.SemaphoreType.DMA((SLOTS,)),
+                pltpu.SemaphoreType.DMA((SLOTS,)),
             ],
             compiler_params=pltpu.CompilerParams(
                 collective_id=0, has_side_effects=True, vmem_limit_bytes=32 * 1024 * 1024
             ),
             name="adjoint_residual",
         )(
-            state.reshape(5, 128, 128),
-            adjoint.reshape(5, 128, 128),
-            metric.reshape(9, 128, 128),
-            jacobian.reshape(128, 128),
-            boundary_kind_code.reshape(8, 32),
-            orient.reshape(24, 32),
+            *(
+                pltpu.with_memory_space_constraint(value, pltpu.HBM)
+                for value in (
+                    state.reshape(5, 128, 128),
+                    adjoint.reshape(5, 128, 128),
+                    metric.reshape(9, 128, 128),
+                    jacobian.reshape(128, 128),
+                    boundary_kind_code.reshape(8, 32),
+                    orient.reshape(24, 32),
+                )
+            )
         )
         return out.reshape(5, 8, 16, 128)
 

time: 22.7 us -> 16.9 us (0.74); the launches traced: 22.4 us -> 16.8 us
  local copies, waits for them, and re-layouts: 5.97 us -> 0.73 us
  Pallas kernels: 16.4 us -> 16.1 us
    unnamed x13 -> x1, local copies, waits for them, and re-layouts: 5.97 us -> 0.73 us
    pallas_call x1, Pallas kernels: 16.4 us -> 16.1 us  [body(): pl.pallas_call(lambda *refs: kernel(nx, ny, *refs), out_shape=jax.ShapeDt...]
where the time goes in v1:
time: 16.9 us; the launch traced here: 16.8 us
  Pallas kernels  16.1 us (95%)
  local copies, waits for them, and re-layouts  0.73 us (4%)
    pallas_call x1, Pallas kernels, body(): pl.pallas_call(lambda *refs: kernel(nx, ny, *refs), out_shape=jax.ShapeDt...  16.1 us
    unnamed x1, local copies, waits for them, and re-layouts  0.73 us

profile of v1, /device:TPU:36, one launch (start us, length us, event | category | flops | bytes accessed | tf_op | source)
XLA Modules:
  0.0 16.8 jit_solution(16353104985579138380)
XLA Ops:
  0.0 16.1 %adjoint_residual.1 = f32[5,128,128]{2,1,0:T(8,128)S(1)} custom-call(f32[5,128,128]{2,1,0:T(8,128)} %bitcast.9, f32[5,128,128]{2,1,0:T(8,128)} %bitcast.10, f32[9,128,128]{2,1,0:T(8,128)} %bitcast.8, f32[128,128]{1,0:T(8,128)} %bitcast.11, s32[8,32]{1,0:T(8,128)} %bitcast.13, s32[24,32]{1,0:T(8,128)} %bitcast.12), custom_call_target="tpu_custom_call" | custom-call | tf_op jit(solution)/shard_map/adjoint_residual/pallas_call | solution.py:525
  16.1 0.7 %copy.8 = f32[5,8,16,128]{3,2,1,0:T(8,128)} copy(f32[5,8,16,128]{3,2,1,0:T(8,128)S(1)} %bitcast.7) | data formatting | bytes 655360

commit v2 on v1

--- a/solution.py
+++ b/solution.py
@@ -150,7 +150,7 @@
     nx, ny,
     state_ref, adj_ref, met_ref, jac_ref, code_ref, orient_ref, out_ref,
     st, ad, mt, jc, cd, ori, nb, tb, acc, acct, send, recv, gout, mb, el,
-    load_sem, send_sem, recv_sem,
+    load_sem, send_sem, recv_sem, ready_sem,
 ):
     f32 = jnp.float32
     ix, iy, iz = lax.axis_index("gx"), lax.axis_index("gy"), lax.axis_index("gz")
@@ -160,7 +160,14 @@
         {"gy": lax.max(iy - 1, 0)}, {"gy": lax.min(iy + 1, ny - 1)},
         {"gz": 1 - iz},
     ]
-    edge = [low_x, high_x, low_y, high_y, None]
+    inner_side = [jnp.logical_not(e) for e in (low_x, high_x, low_y, high_y)] + [None]
+    opens = [(ix + 3) % 4 < 2, ix % 4 >= 2, (iy + 3) % 4 != 3, iy % 4 == 3, iz == 0]
+
+    def both(first, second):
+        return second if first is None else first & second
+
+    greets = [both(there, jnp.logical_not(theirs)) for there, theirs in zip(inner_side, opens)]
+    greeted = [both(there, theirs) for there, theirs in zip(inner_side, opens)]
     spans = [(0, 2), (2, 2), (4, 1), (5, 1), (6, 1)]
 
     outer = [pl.ds(0, 16), pl.ds(112, 16)]
@@ -170,28 +177,24 @@
         moves += [(src.at[:, rows], dst.at[:, rows]) for src, dst in ((state_ref, st), (adj_ref, ad))]
         moves += [(jac_ref.at[rows], jc.at[rows]), (met_ref.at[0:3, rows], mt.at[0:3, rows])]
     moves += [(src.at[:, inner], dst.at[:, inner]) for src, dst in ((state_ref, st), (adj_ref, ad))]
-    moves += [(jac_ref.at[inner], jc.at[inner]), (met_ref.at[3:9], mt.at[3:9])]
-    moves.append((met_ref.at[0:3, inner], mt.at[0:3, inner]))
+    moves += [(jac_ref.at[inner], jc.at[inner]), (met_ref.at[3:6], mt.at[3:6])]
+    moves += [(met_ref.at[0:3, inner], mt.at[0:3, inner]), (met_ref.at[6:9], mt.at[6:9])]
     loads = [pltpu.make_async_copy(src, dst, load_sem.at[n]) for n, (src, dst) in enumerate(moves)]
     barrier = pltpu.get_barrier_semaphore()
     for side in range(5):
-        def greet(side=side):
+        @pl.when(greets[side])
+        def _(side=side):
             pl.semaphore_signal(barrier, inc=1, device_id=ids[side], device_id_type=MESH)
 
-        if edge[side] is None:
-            greet()
-        else:
-            pl.when(jnp.logical_not(edge[side]))(greet)
     for copy in loads:
         copy.start()
     for side in range(4):
-        if edge[side] is not None:
-            @pl.when(edge[side])
-            def _(side=side):
-                first, count = spans[side]
-                for slot in range(first, first + count):
-                    for n in range(13):
-                        recv[slot, n] = jnp.zeros((8, 128), f32)
+        @pl.when(jnp.logical_not(inner_side[side]))
+        def _(side=side):
+            first, count = spans[side]
+            for slot in range(first, first + count):
+                for n in range(13):
+                    recv[slot, n] = jnp.zeros((8, 128), f32)
 
     sub = lax.broadcasted_iota(jnp.int32, (8, 128), 0)
     lane = lax.broadcasted_iota(jnp.int32, (8, 128), 1)
@@ -255,7 +258,7 @@
     flag_y_top = (y_rows(16, 3) > 0.5) & jnp.logical_not(high_y)
     flag_z_top = (jnp.broadcast_to(flag_z[31:32], (8, 128)) > 0.5) & jnp.logical_not(low_row) & (iz == 0)
 
-    def convert(rows):
+    def convert(rows, keep=True):
         rho, m, energy = st[0, rows], [st[n, rows] for n in (1, 2, 3)], st[4, rows]
         r = rcp(rho)
         v = [x * r for x in m]
@@ -265,8 +268,9 @@
         w = [ad[n, rows] * rj for n in range(5)]
         w[4] = 0.5 * w[4]
         values = [rho, *v, beta, *node_extras(rho, beta, 0.5 * r, pressure * r), *w]
-        for n, value in enumerate(values):
-            nb[n, rows] = value
+        if keep:
+            for n, value in enumerate(values):
+                nb[n, rows] = value
         return values
 
     for load in loads[2:10]:
@@ -286,11 +290,6 @@
             pack(slot, raw)
         else:
             pack(slot, raw, flag_x_top[slot - 2], flip_sub)
-
-    waits = lax.convert_element_type(
-        5 - jnp.where(low_x, 1, 0) - jnp.where(high_x, 1, 0) - jnp.where(low_y, 1, 0) - jnp.where(high_y, 1, 0), jnp.int32
-    )
-    pl.semaphore_wait(barrier, waits)
 
     landing = [1, 0, 3, 2, 4]
     def copy_of(side, place):
@@ -307,38 +306,71 @@
     copies = [[copy_of(side, place) for place in range(spans[side][1])] for side in range(5)]
 
     def on_side(side, act):
-        if edge[side] is None:
+        if inner_side[side] is None:
             act()
         else:
-            pl.when(jnp.logical_not(edge[side]))(act)
-
-    for place in range(2):
-        for side in (0, 1):
-            on_side(side, copies[side][place].start)
-
-    for load in loads[10:13]:
+            pl.when(inner_side[side])(act)
+
+    def start(side):
+        for copy in copies[side]:
+            copy.start()
+
+    arrivals = sum(jnp.where(here, 1, 0) for here in greeted)
+
+    @pl.when(arrivals > 0)
+    def _():
+        pl.semaphore_wait(barrier, arrivals)
+
+    for side in range(5):
+        @pl.when(greeted[side])
+        def _(side=side):
+            pl.semaphore_signal(ready_sem.at[landing[side]], inc=1, device_id=ids[side], device_id_type=MESH)
+
+    for side in (1, 0):
+        pl.when(greeted[side])(lambda side=side: start(side))
+
+    for load in loads[10:14]:
         load.wait()
+    for slot, y, flag in ((4, 0, None), (5, 15, flag_y_top)):
+        rows = pl.ds(y, 8, stride=16)
+        values = convert(rows, keep=False)
+        pack(slot, values[0:5] + values[9:14] + [mt[3 + n, rows] for n in range(3)], flag, flip_sub)
+    for side in (2, 3):
+        pl.when(greeted[side])(lambda side=side: start(side))
 
     @pl.loop(2, 14)
     def _(block):
         convert(pl.ds(pl.multiple_of(block * 8, 8), 8))
 
-    loads[13].wait()
-
     def load_y(y):
         rows = pl.ds(y, 8, stride=16)
         return [nb[n, rows] for n in range(14)] + [mt[3 + n, rows] for n in range(3)]
 
-    for slot, y in ((4, 0), (5, 15)):
-        values = load_y(y)
-        raw = values[0:5] + values[9:17]
-        if slot == 4:
-            pack(slot, raw)
-        else:
-            pack(slot, raw, flag_y_top, flip_sub)
-    on_side(2, copies[2][0].start)
-    on_side(3, copies[3][0].start)
-
+    loads[14].wait()
+
+    def load_x(rows):
+        return [nb[n, rows] for n in range(14)] + [mt[n, rows] for n in range(3)]
+
+    @pl.loop(0, 4)
+    def _(chunk):
+        base = (chunk // 2) * 64 + (chunk % 2) * 8
+
+        def at(a):
+            return pl.ds(pl.multiple_of(base + a * 16, 8), 8)
+
+        def store(a, total):
+            for n in range(5):
+                acc[n, at(a)] = total[n]
+
+        line(lambda a: load_x(at(a)), store)
+
+    for side in (1, 0, 2, 3):
+        @pl.when(greets[side])
+        def _(side=side):
+            pl.semaphore_wait(ready_sem.at[side], 1)
+            start(side)
+
+    loads[15].wait()
     for n in range(5):
         tb[n, 0:128] = jnp.transpose(nb[n])
         tb[9 + n, 0:128] = jnp.transpose(nb[9 + n])
@@ -348,6 +380,11 @@
     low_z = [jnp.broadcast_to(tb[n, 0:1], (8, 128)) for n in raw_t]
     high_z = [jnp.broadcast_to(tb[n, 127:128], (8, 128)) for n in raw_t]
     pack(6, [jnp.where(low_row, x, y) for x, y in zip(low_z, high_z)], flag_z_top, flip_lane)
+
+    @pl.when(greets[4])
+    def _():
+        pl.semaphore_wait(ready_sem.at[4], 1)
+
     copies[4][0].start()
 
     @pl.loop(0, 16)
@@ -356,24 +393,6 @@
         rho, beta = tb[0, rows], tb[4, rows]
         for n, value in enumerate(node_extras(rho, beta, 0.5 * rcp(rho), 0.5 * rcp(beta))):
             tb[5 + n, rows] = value
-
-    loads[14].wait()
-
-    def load_x(rows):
-        return [nb[n, rows] for n in range(14)] + [mt[n, rows] for n in range(3)]
-
-    @pl.loop(0, 4)
-    def _(chunk):
-        base = (chunk // 2) * 64 + (chunk % 2) * 8
-
-        def at(a):
-            return pl.ds(pl.multiple_of(base + a * 16, 8), 8)
-
-        def store(a, total):
-            for n in range(5):
-                acc[n, at(a)] = total[n]
-
-        line(lambda a: load_x(at(a)), store)
 
     def add(ref, rows, parts):
         for n in range(5):
@@ -499,7 +518,7 @@
         rows = pl.ds(pl.multiple_of(block * 8, 8), 8)
         finish(rows, [acc[n, rows] for n in range(5)])
 
-    for slot in (0, 2, 1, 3):
+    for slot in (2, 3, 0, 1):
         on_side(slot // 2, copies[landing[slot // 2]][slot % 2].wait_recv)
 
         rows = pl.ds((slot // 2) * 112 + (slot % 2) * 8, 8)
@@ -543,9 +562,10 @@
                 vmem((3, 5, 8, 128), f32),
                 vmem((SLOTS, 3, 8, 128), f32),
                 vmem((32, 32), f32),
-                pltpu.SemaphoreType.DMA((15,)),
+                pltpu.SemaphoreType.DMA((16,)),
                 pltpu.SemaphoreType.DMA((SLOTS,)),
                 pltpu.SemaphoreType.DMA((SLOTS,)),
+                pltpu.SemaphoreType.REGULAR((5,)),
             ],
             compiler_params=pltpu.CompilerParams(
                 collective_id=0, has_side_effects=True, vmem_limit_bytes=32 * 1024 * 1024

time: 16.9 us -> 14.7 us (0.87)
  the two profiles are of different devices: /device:TPU:36 before, /device:TPU:30 now
where the time goes in v2:
time: 14.7 us; the launch traced here: 14.6 us
  Pallas kernels  13.9 us (95%)
  local copies, waits for them, and re-layouts  0.73 us (5%)
    pallas_call x1, Pallas kernels, body(): pl.pallas_call(lambda *refs: kernel(nx, ny, *refs), out_shape=jax.ShapeDt...  13.9 us
    unnamed x1, local copies, waits for them, and re-layouts  0.73 us

profile of v2, /device:TPU:30, one launch (start us, length us, event | category | flops | bytes accessed | tf_op | source)
XLA Modules:
  0.0 14.6 jit_solution(4869348371651196075)
XLA Ops:
  0.0 13.9 %adjoint_residual.1 = f32[5,128,128]{2,1,0:T(8,128)S(1)} custom-call(f32[5,128,128]{2,1,0:T(8,128)} %bitcast.9, f32[5,128,128]{2,1,0:T(8,128)} %bitcast.10, f32[9,128,128]{2,1,0:T(8,128)} %bitcast.8, f32[128,128]{1,0:T(8,128)} %bitcast.11, s32[8,32]{1,0:T(8,128)} %bitcast.13, s32[24,32]{1,0:T(8,128)} %bitcast.12), custom_call_target="tpu_custom_call" | custom-call | tf_op jit(solution)/shard_map/adjoint_residual/pallas_call | solution.py:544
  13.9 0.7 %copy.8 = f32[5,8,16,128]{3,2,1,0:T(8,128)} copy(f32[5,8,16,128]{3,2,1,0:T(8,128)S(1)} %bitcast.7) | data formatting | bytes 655360

commit v3 on v2

--- a/solution.py
+++ b/solution.py
@@ -131,6 +131,12 @@
     return [0.5 * jnp.log(rho), 0.5 * jnp.log(beta), inv_rho, inv_beta]
 
 
+def primitives(u):
+    v = [x * rcp(u[0]) for x in u[1:4]]
+    pressure = 0.4 * (u[4] - 0.5 * dot3(u[1:4], v))
+    return [u[0], *v, (0.5 * u[0]) * rcp(pressure)]
+
+
 def line(load, store):
     total = [None] * 4
     for a in range(4):
@@ -150,7 +156,8 @@
     nx, ny,
     state_ref, adj_ref, met_ref, jac_ref, code_ref, orient_ref, out_ref,
     st, ad, mt, jc, cd, ori, nb, tb, acc, acct, send, recv, gout, mb, el,
-    load_sem, send_sem, recv_sem, ready_sem,
+    send_w, recv_u, recv_g, recv_w, recv_f, xo,
+    load_sem, send_sem, recv_sem, x_send_sem, x_recv_sem, ready_sem,
 ):
     f32 = jnp.float32
     ix, iy, iz = lax.axis_index("gx"), lax.axis_index("gy"), lax.axis_index("gz")
@@ -168,7 +175,7 @@
 
     greets = [both(there, jnp.logical_not(theirs)) for there, theirs in zip(inner_side, opens)]
     greeted = [both(there, theirs) for there, theirs in zip(inner_side, opens)]
-    spans = [(0, 2), (2, 2), (4, 1), (5, 1), (6, 1)]
+    place = [None, None, 0, 1, 2]
 
     outer = [pl.ds(0, 16), pl.ds(112, 16)]
     inner = pl.ds(16, 96)
@@ -191,10 +198,72 @@
     for side in range(4):
         @pl.when(jnp.logical_not(inner_side[side]))
         def _(side=side):
-            first, count = spans[side]
-            for slot in range(first, first + count):
+            blank = jnp.zeros((8, 128), f32)
+            if side < 2:
+                for ref, count in ((recv_u, 5), (recv_g, 3), (recv_w, 5)):
+                    for n in range(count):
+                        for half in range(2):
+                            ref[side, n, pl.ds(8 * half, 8)] = blank
+                if side == 0:
+                    recv_f[...] = jnp.zeros((8, 32), jnp.int32)
+            else:
                 for n in range(13):
-                    recv[slot, n] = jnp.zeros((8, 128), f32)
+                    recv[place[side], n] = blank
+
+    landing = [1, 0, 3, 2, 4]
+    ends = [pl.ds(0, 16), pl.ds(112, 16)]
+
+    def remote(source, target, sent, received, side):
+        return pltpu.make_async_remote_copy(
+            src_ref=source, dst_ref=target, send_sem=sent, recv_sem=received,
+            device_id=ids[side], device_id_type=MESH,
+        )
+
+    def x_copy(side, n, source, target):
+        return remote(source, target, x_send_sem.at[4 * side + n], x_recv_sem.at[4 * landing[side] + n], side)
+
+    raw_copies, weight_copies = [], []
+    for side in range(2):
+        to = landing[side]
+        raw_copies.append(
+            [
+                x_copy(side, 0, state_ref.at[:, ends[side]], recv_u.at[to]),
+                x_copy(side, 1, met_ref.at[0:3, ends[side]], recv_g.at[to]),
+            ]
+        )
+        weight_copies.append(x_copy(side, 2, send_w.at[side], recv_w.at[to]))
+    flag_copy = x_copy(1, 3, orient_ref.at[0:8], recv_f)
+    raw_copies[1].insert(0, flag_copy)
+    copies = {
+        side: remote(
+            send.at[place[side]], recv.at[place[landing[side]]],
+            send_sem.at[place[side]], recv_sem.at[place[landing[side]]], side,
+        )
+        for side in (2, 3, 4)
+    }
+
+    def on_side(side, act):
+        if inner_side[side] is None:
+            act()
+        else:
+            pl.when(inner_side[side])(act)
+
+    def start_raw(side):
+        for copy in raw_copies[side]:
+            copy.start()
+
+    arrivals = sum(jnp.where(here, 1, 0) for here in greeted)
+
+    @pl.when(arrivals > 0)
+    def _():
+        pl.semaphore_wait(barrier, arrivals)
+
+    for side in (1, 0):
+        pl.when(greeted[side])(lambda side=side: start_raw(side))
+    for side in range(5):
+        @pl.when(greeted[side])
+        def _(side=side):
+            pl.semaphore_signal(ready_sem.at[landing[side]], inc=1, device_id=ids[side], device_id_type=MESH)
 
     sub = lax.broadcasted_iota(jnp.int32, (8, 128), 0)
     lane = lax.broadcasted_iota(jnp.int32, (8, 128), 1)
@@ -253,7 +322,8 @@
         mb[slot, 1] = far
         mb[slot, 2] = at_edge[slot] - far
     flag_x_mid = [x_rows(8, 0, half) > 0.5 for half in range(2)]
-    flag_x_top = [(x_rows(8, 1, half) > 0.5) & jnp.logical_not(high_x) for half in range(2)]
+    for half in range(2):
+        mb[2 + half, 3] = x_rows(8, 1, half)
     flag_y_mid = [y_rows(16, ey) > 0.5 for ey in range(3)]
     flag_y_top = (y_rows(16, 3) > 0.5) & jnp.logical_not(high_y)
     flag_z_top = (jnp.broadcast_to(flag_z[31:32], (8, 128)) > 0.5) & jnp.logical_not(low_row) & (iz == 0)
@@ -282,61 +352,21 @@
                 value = jnp.where(flag, flip(value), value)
             send[slot, n] = value
 
-    for slot, block in ((0, 0), (1, 1), (2, 14), (3, 15)):
-        rows = pl.ds(block * 8, 8)
-        values = convert(rows)
-        raw = values[0:5] + values[9:14] + [mt[n, rows] for n in range(3)]
-        if slot < 2:
-            pack(slot, raw)
-        else:
-            pack(slot, raw, flag_x_top[slot - 2], flip_sub)
-
-    landing = [1, 0, 3, 2, 4]
-    def copy_of(side, place):
-        source, target = spans[side][0] + place, spans[landing[side]][0] + place
-        return pltpu.make_async_remote_copy(
-            src_ref=send.at[source],
-            dst_ref=recv.at[target],
-            send_sem=send_sem.at[source],
-            recv_sem=recv_sem.at[target],
-            device_id=ids[side],
-            device_id_type=MESH,
-        )
-
-    copies = [[copy_of(side, place) for place in range(spans[side][1])] for side in range(5)]
-
-    def on_side(side, act):
-        if inner_side[side] is None:
-            act()
-        else:
-            pl.when(inner_side[side])(act)
-
-    def start(side):
-        for copy in copies[side]:
-            copy.start()
-
-    arrivals = sum(jnp.where(here, 1, 0) for here in greeted)
-
-    @pl.when(arrivals > 0)
-    def _():
-        pl.semaphore_wait(barrier, arrivals)
-
-    for side in range(5):
-        @pl.when(greeted[side])
-        def _(side=side):
-            pl.semaphore_signal(ready_sem.at[landing[side]], inc=1, device_id=ids[side], device_id_type=MESH)
-
+    for slot, block in ((2, 14), (3, 15), (0, 0), (1, 1)):
+        values = convert(pl.ds(block * 8, 8))
+        for n in range(5):
+            send_w[slot // 2, n, pl.ds(8 * (slot % 2), 8)] = values[9 + n]
     for side in (1, 0):
-        pl.when(greeted[side])(lambda side=side: start(side))
+        pl.when(greeted[side])(weight_copies[side].start)
 
     for load in loads[10:14]:
         load.wait()
-    for slot, y, flag in ((4, 0, None), (5, 15, flag_y_top)):
+    for slot, y, flag in ((0, 0, None), (1, 15, flag_y_top)):
         rows = pl.ds(y, 8, stride=16)
         values = convert(rows, keep=False)
         pack(slot, values[0:5] + values[9:14] + [mt[3 + n, rows] for n in range(3)], flag, flip_sub)
     for side in (2, 3):
-        pl.when(greeted[side])(lambda side=side: start(side))
+        pl.when(greeted[side])(copies[side].start)
 
     @pl.loop(2, 14)
     def _(block):
@@ -364,11 +394,15 @@
 
         line(lambda a: load_x(at(a)), store)
 
-    for side in (1, 0, 2, 3):
+    for side in (2, 3, 1, 0):
         @pl.when(greets[side])
         def _(side=side):
             pl.semaphore_wait(ready_sem.at[side], 1)
-            start(side)
+            if side < 2:
+                start_raw(side)
+                weight_copies[side].start()
+            else:
+                copies[side].start()
 
     loads[15].wait()
     for n in range(5):
@@ -379,13 +413,13 @@
     raw_t = [0, 1, 2, 3, 4, 9, 10, 11, 12, 13, 14, 15, 16]
     low_z = [jnp.broadcast_to(tb[n, 0:1], (8, 128)) for n in raw_t]
     high_z = [jnp.broadcast_to(tb[n, 127:128], (8, 128)) for n in raw_t]
-    pack(6, [jnp.where(low_row, x, y) for x, y in zip(low_z, high_z)], flag_z_top, flip_lane)
+    pack(2, [jnp.where(low_row, x, y) for x, y in zip(low_z, high_z)], flag_z_top, flip_lane)
 
     @pl.when(greets[4])
     def _():
         pl.semaphore_wait(ready_sem.at[4], 1)
 
-    copies[4][0].start()
+    copies[4].start()
 
     @pl.loop(0, 16)
     def _(block):
@@ -451,46 +485,47 @@
         add(acct, upper, to_u)
 
     for side in (4, 2, 3):
-        on_side(side, copies[landing[side]][0].wait_recv)
+        on_side(side, copies[landing[side]].wait_recv)
     for n in range(13):
-        recv[6, n] = pltpu.roll(recv[6, n], 1, 0)
+        recv[2, n] = pltpu.roll(recv[2, n], 1, 0)
 
     inflow = np.array(INFLOW_STATE)
     inflow_v = inflow[1:4] / inflow[0]
     inflow_p = 0.4 * (inflow[4] - 0.5 * np.sum(inflow[1:4] * inflow_v))
     far_values = [float(inflow[0]), *[float(x) for x in inflow_v], float(inflow[0] / (2.0 * inflow_p))]
 
-    def side_faces(slot):
+    def mirror(v, g, turn):
+        along = turn * dot3(v, g)
+        return [x - along * y for x, y in zip(v, g)]
+
+    def outer_node(slot, own, prim, normal):
+        is_far, is_wall = mb[slot, 1] > 0.5, mb[slot, 2] > 0.5
+        outside = is_far | is_wall
+        g = own[14:17]
+        image = [own[0], *mirror(own[1:4], g, 2.0 * rcp(dot3(g, g))), own[4]]
+        prim = [jnp.where(is_far, f, jnp.where(is_wall, i, o)) for f, i, o in zip(far_values, image, prim)]
+        normal = [jnp.where(outside, i, o) for i, o in zip(g, normal)]
+        extras = node_extras(prim[0], prim[4], 0.5 * rcp(prim[0]), 0.5 * rcp(prim[4]))
+        return [*prim, *extras], normal
+
+    def side_faces(slot, own, other, w, normal):
+        is_wall = mb[slot, 2] > 0.5
+        outside = (mb[slot, 1] > 0.5) | is_wall
+        w = [jnp.where(outside, 0.0, x) for x in w]
+        mine, theirs = pair(own, [*other, *w, *normal], mb[slot, 0], face=True)
+        g = own[14:17]
+        back = [theirs[0], *mirror(theirs[1:4], g, 2.0 * rcp(dot3(g, g))), theirs[4]]
+        return [x + jnp.where(is_wall, y, 0.0) for x, y in zip(mine, back)]
+
+    @pl.loop(0, 3)
+    def _(slot):
         own = [send[slot, n] for n in range(13)]
         other = [recv[slot, n] for n in range(13)]
-        scale, far, wall = mb[slot, 0], mb[slot, 1], mb[slot, 2]
-        is_far, is_wall = far > 0.5, wall > 0.5
-        outside = is_far | is_wall
-        g = own[10:13]
-        turn = 2.0 * rcp(dot3(g, g))
-
-        def mirror(v):
-            along = turn * dot3(v, g)
-            return [x - along * y for x, y in zip(v, g)]
-
-        image = [own[0], *mirror(own[1:4]), own[4]]
-        oth = [
-            jnp.where(is_far, f, jnp.where(is_wall, i, o)) for f, i, o in zip(far_values, image, other[0:5])
-        ]
-        oth_w = [jnp.where(outside, 0.0, o) for o in other[5:10]]
-        oth_g = [jnp.where(outside, i, o) for i, o in zip(g, other[10:13])]
-
-        def full(prim, w, normal):
-            return [*prim, *node_extras(prim[0], prim[4], 0.5 * rcp(prim[0]), 0.5 * rcp(prim[4])), *w, *normal]
-
-        mine, theirs = pair(full(own[0:5], own[5:10], g), full(oth, oth_w, oth_g), scale, face=True)
-        back = [theirs[0], *mirror(theirs[1:4]), theirs[4]]
-        return [x + jnp.where(is_wall, y, 0.0) for x, y in zip(mine, back)]
-
-    @pl.loop(4, SLOTS)
-    def _(slot):
-        for n, part in enumerate(side_faces(slot)):
-            gout[slot - 4, n] = part
+        extras = node_extras(own[0], own[4], 0.5 * rcp(own[0]), 0.5 * rcp(own[4]))
+        own = [*own[0:5], *extras, *own[5:13]]
+        prim, normal = outer_node(slot + 4, own, other[0:5], other[10:13])
+        for n, part in enumerate(side_faces(slot + 4, own, prim, other[5:10], normal)):
+            gout[slot, n] = part
 
     add(acc, pl.ds(0, 8, stride=16), [gout[0, n] for n in range(5)])
     add(acc, pl.ds(15, 8, stride=16), flipped([gout[1, n] for n in range(5)], flag_y_top, flip_sub))
@@ -518,17 +553,47 @@
         rows = pl.ds(pl.multiple_of(block * 8, 8), 8)
         finish(rows, [acc[n, rows] for n in range(5)])
 
-    for slot in (2, 3, 0, 1):
-        on_side(slot // 2, copies[landing[slot // 2]][slot % 2].wait_recv)
-
-        rows = pl.ds((slot // 2) * 112 + (slot % 2) * 8, 8)
-        parts = side_faces(slot)
-        if slot >= 2:
-            parts = flipped(parts, flag_x_top[slot - 2], flip_sub)
-        finish(rows, [acc[n, rows] + part for n, part in enumerate(parts)])
-
-    for side in (4, 2, 3, 0, 1):
-        for copy in copies[side]:
+    def x_rows_of(side, half):
+        return pl.ds(side * 112 + half * 8, 8)
+
+    def x_flags(side, half):
+        return mb[2 * side + half, 3] > 0.5
+
+    on_side(0, flag_copy.wait_recv)
+    el[0:8, :] = recv_f[...].astype(f32)
+    below = jnp.dot(el[0:8, :], spread, preferred_element_type=f32)
+    for half in range(2):
+        mb[half, 3] = jnp.where(
+            sub < 4,
+            jnp.broadcast_to(below[4 + 2 * half : 5 + 2 * half], (8, 128)),
+            jnp.broadcast_to(below[5 + 2 * half : 6 + 2 * half], (8, 128)),
+        )
+
+    for side in (1, 0):
+        for copy in raw_copies[landing[side]][-2:]:
+            on_side(side, copy.wait_recv)
+        for half in range(2):
+            rows, flag = pl.ds(8 * half, 8), x_flags(side, half)
+            u = flipped([recv_u[side, n, rows] for n in range(5)], flag, flip_sub)
+            normal = flipped([recv_g[side, n, rows] for n in range(3)], flag, flip_sub)
+            prim = primitives(u)
+            other, normal = outer_node(2 * side + half, load_x(x_rows_of(side, half)), prim, normal)
+            for n, value in enumerate([*other, *normal]):
+                xo[2 * side + half, n] = value
+
+    for side in (1, 0):
+        on_side(side, weight_copies[landing[side]].wait_recv)
+        for half in range(2):
+            slot, rows = 2 * side + half, x_rows_of(side, half)
+            w = flipped([recv_w[side, n, pl.ds(8 * half, 8)] for n in range(5)], x_flags(side, half), flip_sub)
+            other, normal = [xo[slot, n] for n in range(9)], [xo[slot, 9 + n] for n in range(3)]
+            parts = side_faces(slot, load_x(rows), other, w, normal)
+            finish(rows, [acc[n, rows] + part for n, part in enumerate(parts)])
+
+    for side in (4, 2, 3):
+        on_side(side, copies[side].wait_send)
+    for side in (1, 0):
+        for copy in (*raw_copies[side], weight_copies[side]):
             on_side(side, copy.wait_send)
 
 
@@ -557,14 +622,22 @@
                 vmem((17, 136, 128), f32),
                 vmem((5, 128, 128), f32),
                 vmem((5, 136, 128), f32),
-                vmem((SLOTS, 13, 8, 128), f32),
-                vmem((SLOTS, 13, 8, 128), f32),
+                vmem((3, 13, 8, 128), f32),
+                vmem((3, 13, 8, 128), f32),
                 vmem((3, 5, 8, 128), f32),
-                vmem((SLOTS, 3, 8, 128), f32),
+                vmem((SLOTS, 4, 8, 128), f32),
                 vmem((32, 32), f32),
+                vmem((2, 5, 16, 128), f32),
+                vmem((2, 5, 16, 128), f32),
+                vmem((2, 3, 16, 128), f32),
+                vmem((2, 5, 16, 128), f32),
+                vmem((8, 32), jnp.int32),
+                vmem((4, 12, 8, 128), f32),
                 pltpu.SemaphoreType.DMA((16,)),
-                pltpu.SemaphoreType.DMA((SLOTS,)),
-                pltpu.SemaphoreType.DMA((SLOTS,)),
+                pltpu.SemaphoreType.DMA((3,)),
+                pltpu.SemaphoreType.DMA((3,)),
+                pltpu.SemaphoreType.DMA((8,)),
+                pltpu.SemaphoreType.DMA((8,)),
                 pltpu.SemaphoreType.REGULAR((5,)),
             ],
             compiler_params=pltpu.CompilerParams(

time: 14.7 us -> 13.3 us (0.905)
  Pallas kernels: 13.9 us -> 12.5 us
    pallas_call x1, Pallas kernels: 13.9 us -> 12.5 us  [body(): pl.pallas_call(lambda *refs: kernel(nx, ny, *refs), out_shape=jax.ShapeDt...]
where the time goes in v3:
time: 13.3 us; the launch traced here: 13.2 us
  Pallas kernels  12.5 us (94%)
  local copies, waits for them, and re-layouts  0.73 us (5%)
    pallas_call x1, Pallas kernels, body(): pl.pallas_call(lambda *refs: kernel(nx, ny, *refs), out_shape=jax.ShapeDt...  12.5 us
    unnamed x1, local copies, waits for them, and re-layouts  0.73 us

profile of v3, /device:TPU:30, one launch (start us, length us, event | category | flops | bytes accessed | tf_op | source)
XLA Modules:
  0.0 13.2 jit_solution(8861466136023131265)
XLA Ops:
  0.0 12.5 %adjoint_residual.1 = f32[5,128,128]{2,1,0:T(8,128)S(1)} custom-call(f32[5,128,128]{2,1,0:T(8,128)} %bitcast.9, f32[5,128,128]{2,1,0:T(8,128)} %bitcast.10, f32[9,128,128]{2,1,0:T(8,128)} %bitcast.8, f32[128,128]{1,0:T(8,128)} %bitcast.11, s32[8,32]{1,0:T(8,128)} %bitcast.13, s32[24,32]{1,0:T(8,128)} %bitcast.12), custom_call_target="tpu_custom_call" | custom-call | tf_op jit(solution)/shard_map/adjoint_residual/pallas_call | solution.py:609
  12.5 0.7 %copy.8 = f32[5,8,16,128]{3,2,1,0:T(8,128)} copy(f32[5,8,16,128]{3,2,1,0:T(8,128)S(1)} %bitcast.7) | data formatting | bytes 655360

commit v4 on v3

--- a/solution.py
+++ b/solution.py
@@ -394,15 +394,19 @@
 
         line(lambda a: load_x(at(a)), store)
 
-    for side in (2, 3, 1, 0):
-        @pl.when(greets[side])
-        def _(side=side):
+    def answered(side, here):
+        @pl.when(greets[side] & here)
+        def _():
             pl.semaphore_wait(ready_sem.at[side], 1)
             if side < 2:
                 start_raw(side)
                 weight_copies[side].start()
             else:
                 copies[side].start()
+
+    answered(2, iy >= 0)
+    answered(3, iy >= 0)
+    answered(0, ix % 4 == 3)
 
     loads[15].wait()
     for n in range(5):
@@ -455,6 +459,8 @@
         add(acc, pl.ds(4 * ey + 3, 8, stride=16), flipped(to_l, flag_y_mid[ey], flip_sub))
         add(acc, pl.ds(4 * ey + 4, 8, stride=16), to_u)
 
+    answered(1, ix % 4 == 0)
+
     def rows_z(chunk, a):
         return pl.ds(chunk * 32 + a, 8, stride=4)
 
@@ -469,6 +475,7 @@
 
         line(lambda a: load_z(rows_z(chunk, a)), store)
 
+    answered(1, ix % 4 == 1)
     for chunk in range(4):
         flag = flag_z[8 * chunk : 8 * chunk + 8] > 0.5
         lower = rows_z(chunk, 3)
@@ -483,6 +490,8 @@
             to_u = [jnp.where(inside, x, 0.0) for x in to_u]
         add(acct, lower, to_l)
         add(acct, upper, to_u)
+
+    answered(0, ix % 4 == 0)
 
     for side in (4, 2, 3):
         on_side(side, copies[landing[side]].wait_recv)

time: 13.3 us -> 13.5 us (1.015); the launches traced: 13.2 us -> 13.2 us
  no operation moved by 1% of the time
where the time goes in v4:
time: 13.5 us; the launch traced here: 13.2 us
  Pallas kernels  12.5 us (93%)
  local copies, waits for them, and re-layouts  0.73 us (5%)
    pallas_call x1, Pallas kernels, body(): pl.pallas_call(lambda *refs: kernel(nx, ny, *refs), out_shape=jax.ShapeDt...  12.5 us
    unnamed x1, local copies, waits for them, and re-layouts  0.73 us

profile of v4, /device:TPU:30, one launch (start us, length us, event | category | flops | bytes accessed | tf_op | source)
XLA Modules:
  0.0 13.2 jit_solution(9216899741439146205)
XLA Ops:
  0.0 12.5 %adjoint_residual.1 = f32[5,128,128]{2,1,0:T(8,128)S(1)} custom-call(f32[5,128,128]{2,1,0:T(8,128)} %bitcast.9, f32[5,128,128]{2,1,0:T(8,128)} %bitcast.10, f32[9,128,128]{2,1,0:T(8,128)} %bitcast.8, f32[128,128]{1,0:T(8,128)} %bitcast.11, s32[8,32]{1,0:T(8,128)} %bitcast.13, s32[24,32]{1,0:T(8,128)} %bitcast.12), custom_call_target="tpu_custom_call" | custom-call | tf_op jit(solution)/shard_map/adjoint_residual/pallas_call | solution.py:618
  12.5 0.7 %copy.8 = f32[5,8,16,128]{3,2,1,0:T(8,128)} copy(f32[5,8,16,128]{3,2,1,0:T(8,128)S(1)} %bitcast.7) | data formatting | bytes 655360

commit v5 on v4

--- a/solution.py
+++ b/solution.py
@@ -258,12 +258,13 @@
     def _():
         pl.semaphore_wait(barrier, arrivals)
 
-    for side in (1, 0):
-        pl.when(greeted[side])(lambda side=side: start_raw(side))
     for side in range(5):
         @pl.when(greeted[side])
         def _(side=side):
             pl.semaphore_signal(ready_sem.at[landing[side]], inc=1, device_id=ids[side], device_id_type=MESH)
+
+    for side in (1, 0):
+        pl.when(greeted[side])(lambda side=side: start_raw(side))
 
     sub = lax.broadcasted_iota(jnp.int32, (8, 128), 0)
     lane = lax.broadcasted_iota(jnp.int32, (8, 128), 1)

time: 13.5 us -> 13.5 us (level)
  no operation moved by 1% of the time
where the time goes in v5:
time: 13.5 us; the launch traced here: 13.2 us
  Pallas kernels  12.5 us (93%)
  local copies, waits for them, and re-layouts  0.73 us (5%)
    pallas_call x1, Pallas kernels, body(): pl.pallas_call(lambda *refs: kernel(nx, ny, *refs), out_shape=jax.ShapeDt...  12.5 us
    unnamed x1, local copies, waits for them, and re-layouts  0.73 us

profile of v5, /device:TPU:30, one launch (start us, length us, event | category | flops | bytes accessed | tf_op | source)
XLA Modules:
  0.0 13.2 jit_solution(3970195694215618005)
XLA Ops:
  0.0 12.5 %adjoint_residual.1 = f32[5,128,128]{2,1,0:T(8,128)S(1)} custom-call(f32[5,128,128]{2,1,0:T(8,128)} %bitcast.9, f32[5,128,128]{2,1,0:T(8,128)} %bitcast.10, f32[9,128,128]{2,1,0:T(8,128)} %bitcast.8, f32[128,128]{1,0:T(8,128)} %bitcast.11, s32[8,32]{1,0:T(8,128)} %bitcast.13, s32[24,32]{1,0:T(8,128)} %bitcast.12), custom_call_target="tpu_custom_call" | custom-call | tf_op jit(solution)/shard_map/adjoint_residual/pallas_call | solution.py:619
  12.5 0.7 %copy.8 = f32[5,8,16,128]{3,2,1,0:T(8,128)} copy(f32[5,8,16,128]{3,2,1,0:T(8,128)S(1)} %bitcast.7) | data formatting | bytes 655360

commit v6 on v5

--- a/solution.py
+++ b/solution.py
@@ -168,14 +168,18 @@
         {"gz": 1 - iz},
     ]
     inner_side = [jnp.logical_not(e) for e in (low_x, high_x, low_y, high_y)] + [None]
-    opens = [(ix + 3) % 4 < 2, ix % 4 >= 2, (iy + 3) % 4 != 3, iy % 4 == 3, iz == 0]
-
-    def both(first, second):
-        return second if first is None else first & second
-
-    greets = [both(there, jnp.logical_not(theirs)) for there, theirs in zip(inner_side, opens)]
-    greeted = [both(there, theirs) for there, theirs in zip(inner_side, opens)]
+    below, here = (ix + 3) % 4, ix % 4
+    first = [below >= 2, here < 2, iy % 4 == 0, iy % 4 != 3]
+    tied = [below == 2, here == 2]
+    slow = tied[1] & inner_side[1]
+
     place = [None, None, 0, 1, 2]
+    greets = [there & mine for there, mine in zip(inner_side, first)]
+    greeted = [there & jnp.logical_not(mine) for there, mine in zip(inner_side, first)]
+    early = [greeted[side] & jnp.logical_not(tied[side]) for side in range(2)]
+
+    def count(*flags):
+        return sum(jnp.where(flag, 1, 0) for flag in flags)
 
     outer = [pl.ds(0, 16), pl.ds(112, 16)]
     inner = pl.ds(16, 96)
@@ -188,10 +192,13 @@
     moves += [(met_ref.at[0:3, inner], mt.at[0:3, inner]), (met_ref.at[6:9], mt.at[6:9])]
     loads = [pltpu.make_async_copy(src, dst, load_sem.at[n]) for n, (src, dst) in enumerate(moves)]
     barrier = pltpu.get_barrier_semaphore()
-    for side in range(5):
+    def signal(semaphore, target):
+        pl.semaphore_signal(semaphore, inc=1, device_id=target, device_id_type=MESH)
+
+    for side in range(4):
         @pl.when(greets[side])
         def _(side=side):
-            pl.semaphore_signal(barrier, inc=1, device_id=ids[side], device_id_type=MESH)
+            signal(barrier, {**ids[side], "gz": jnp.where(tied[side], 0, 1) if side < 2 else 0})
 
     for copy in loads:
         copy.start()
@@ -252,19 +259,41 @@
         for copy in raw_copies[side]:
             copy.start()
 
-    arrivals = sum(jnp.where(here, 1, 0) for here in greeted)
-
-    @pl.when(arrivals > 0)
+    def answer(side, core):
+        signal(ready_sem.at[landing[side]], {**ids[side], "gz": core})
+
+    @pl.when(iz == 1)
     def _():
-        pl.semaphore_wait(barrier, arrivals)
-
-    for side in range(5):
-        @pl.when(greeted[side])
-        def _(side=side):
-            pl.semaphore_signal(ready_sem.at[landing[side]], inc=1, device_id=ids[side], device_id_type=MESH)
-
-    for side in (1, 0):
-        pl.when(greeted[side])(lambda side=side: start_raw(side))
+        @pl.when(early[0] | early[1])
+        def _():
+            pl.semaphore_wait(barrier, 2 * count(early[0], early[1]))
+
+        signal(barrier, {"gz": 0})
+        for side in (1, 0):
+            @pl.when(early[side])
+            def _(side=side):
+                answer(side, 1)
+                start_raw(side)
+
+    def meet():
+        pl.semaphore_wait(barrier, 2 * count(slow, greeted[2], greeted[3]) + 1)
+        for side in (1, 0):
+            @pl.when(early[side])
+            def _(side=side):
+                answer(side, 0)
+
+        signal(ready_sem.at[4], {"gz": 1})
+        for side in (1, 2, 3):
+            @pl.when(slow if side == 1 else greeted[side])
+            def _(side=side):
+                answer(side, 0)
+                answer(side, 1)
+
+    @pl.when((iz == 0) & jnp.logical_not(slow))
+    def _():
+        meet()
+        for side in (1, 0):
+            pl.when(early[side])(lambda side=side: start_raw(side))
 
     sub = lax.broadcasted_iota(jnp.int32, (8, 128), 0)
     lane = lax.broadcasted_iota(jnp.int32, (8, 128), 1)
@@ -357,8 +386,9 @@
         values = convert(pl.ds(block * 8, 8))
         for n in range(5):
             send_w[slot // 2, n, pl.ds(8 * (slot % 2), 8)] = values[9 + n]
+    prompt = (iz == 1) | jnp.logical_not(slow)
     for side in (1, 0):
-        pl.when(greeted[side])(weight_copies[side].start)
+        pl.when(early[side] & prompt)(weight_copies[side].start)
 
     for load in loads[10:14]:
         load.wait()
@@ -366,8 +396,9 @@
         rows = pl.ds(y, 8, stride=16)
         values = convert(rows, keep=False)
         pack(slot, values[0:5] + values[9:14] + [mt[3 + n, rows] for n in range(3)], flag, flip_sub)
+
     for side in (2, 3):
-        pl.when(greeted[side])(copies[side].start)
+        pl.when(greeted[side] & (iz == 0) & prompt)(copies[side].start)
 
     @pl.loop(2, 14)
     def _(block):
@@ -405,9 +436,25 @@
             else:
                 copies[side].start()
 
-    answered(2, iy >= 0)
-    answered(3, iy >= 0)
-    answered(0, ix % 4 == 3)
+    @pl.when(iz == 1)
+    def _():
+        pl.semaphore_wait(ready_sem.at[4], 1)
+
+    pl.when(jnp.logical_not(prompt))(meet)
+    for side in (2, 3):
+        pl.when(greeted[side] & ((iz == 1) | jnp.logical_not(prompt)))(copies[side].start)
+    for side in (1, 0):
+        @pl.when(early[side] & jnp.logical_not(prompt))
+        def _(side=side):
+            start_raw(side)
+            weight_copies[side].start()
+
+    @pl.when(slow)
+    def _():
+        start_raw(1)
+        weight_copies[1].start()
+
+    answered(0, here == 3)
 
     loads[15].wait()
     for n in range(5):
@@ -419,12 +466,8 @@
     low_z = [jnp.broadcast_to(tb[n, 0:1], (8, 128)) for n in raw_t]
     high_z = [jnp.broadcast_to(tb[n, 127:128], (8, 128)) for n in raw_t]
     pack(2, [jnp.where(low_row, x, y) for x, y in zip(low_z, high_z)], flag_z_top, flip_lane)
-
-    @pl.when(greets[4])
-    def _():
-        pl.semaphore_wait(ready_sem.at[4], 1)
-
     copies[4].start()
+    answered(3, here != 2)
 
     @pl.loop(0, 16)
     def _(block):
@@ -460,7 +503,9 @@
         add(acc, pl.ds(4 * ey + 3, 8, stride=16), flipped(to_l, flag_y_mid[ey], flip_sub))
         add(acc, pl.ds(4 * ey + 4, 8, stride=16), to_u)
 
-    answered(1, ix % 4 == 0)
+    answered(3, here == 2)
+    answered(2, iy >= 0)
+    answered(1, here == 0)
 
     def rows_z(chunk, a):
         return pl.ds(chunk * 32 + a, 8, stride=4)
@@ -476,7 +521,7 @@
 
         line(lambda a: load_z(rows_z(chunk, a)), store)
 
-    answered(1, ix % 4 == 1)
+    answered(1, here == 1)
     for chunk in range(4):
         flag = flag_z[8 * chunk : 8 * chunk + 8] > 0.5
         lower = rows_z(chunk, 3)
@@ -492,7 +537,7 @@
         add(acct, lower, to_l)
         add(acct, upper, to_u)
 
-    answered(0, ix % 4 == 0)
+    answered(0, here == 0)
 
     for side in (4, 2, 3):
         on_side(side, copies[landing[side]].wait_recv)
@@ -571,12 +616,12 @@
 
     on_side(0, flag_copy.wait_recv)
     el[0:8, :] = recv_f[...].astype(f32)
-    below = jnp.dot(el[0:8, :], spread, preferred_element_type=f32)
+    below_flags = jnp.dot(el[0:8, :], spread, preferred_element_type=f32)
     for half in range(2):
         mb[half, 3] = jnp.where(
             sub < 4,
-            jnp.broadcast_to(below[4 + 2 * half : 5 + 2 * half], (8, 128)),
-            jnp.broadcast_to(below[5 + 2 * half : 6 + 2 * half], (8, 128)),
+            jnp.broadcast_to(below_flags[4 + 2 * half : 5 + 2 * half], (8, 128)),
+            jnp.broadcast_to(below_flags[5 + 2 * half : 6 + 2 * half], (8, 128)),
         )
 
     for side in (1, 0):

time: 13.5 us -> 12.9 us (0.956)
  the two profiles are of different devices: /device:TPU:30 before, /device:TPU:160 now
where the time goes in v6:
time: 12.9 us; the launch traced here: 12.8 us
  Pallas kernels  12 us (93%)
  local copies, waits for them, and re-layouts  0.73 us (6%)
    pallas_call x1, Pallas kernels, body(): pl.pallas_call(lambda *refs: kernel(nx, ny, *refs), out_shape=jax.ShapeDt...  12 us
    unnamed x1, local copies, waits for them, and re-layouts  0.73 us

profile of v6, /device:TPU:160, one launch (start us, length us, event | category | flops | bytes accessed | tf_op | source)
XLA Modules:
  0.0 12.8 jit_solution(5870369348309705554)
XLA Ops:
  0.0 12.0 %adjoint_residual.1 = f32[5,128,128]{2,1,0:T(8,128)S(1)} custom-call(f32[5,128,128]{2,1,0:T(8,128)} %bitcast.9, f32[5,128,128]{2,1,0:T(8,128)} %bitcast.10, f32[9,128,128]{2,1,0:T(8,128)} %bitcast.8, f32[128,128]{1,0:T(8,128)} %bitcast.11, s32[8,32]{1,0:T(8,128)} %bitcast.13, s32[24,32]{1,0:T(8,128)} %bitcast.12), custom_call_target="tpu_custom_call" | custom-call | tf_op jit(solution)/shard_map/adjoint_residual/pallas_call | solution.py:664
  12.0 0.7 %copy.8 = f32[5,8,16,128]{3,2,1,0:T(8,128)} copy(f32[5,8,16,128]{3,2,1,0:T(8,128)S(1)} %bitcast.7) | data formatting | bytes 655360

commit v7 on v6

--- a/solution.py
+++ b/solution.py
@@ -181,15 +181,8 @@
     def count(*flags):
         return sum(jnp.where(flag, 1, 0) for flag in flags)
 
-    outer = [pl.ds(0, 16), pl.ds(112, 16)]
-    inner = pl.ds(16, 96)
-    moves = [(code_ref, cd), (orient_ref, ori)]
-    for rows in outer:
-        moves += [(src.at[:, rows], dst.at[:, rows]) for src, dst in ((state_ref, st), (adj_ref, ad))]
-        moves += [(jac_ref.at[rows], jc.at[rows]), (met_ref.at[0:3, rows], mt.at[0:3, rows])]
-    moves += [(src.at[:, inner], dst.at[:, inner]) for src, dst in ((state_ref, st), (adj_ref, ad))]
-    moves += [(jac_ref.at[inner], jc.at[inner]), (met_ref.at[3:6], mt.at[3:6])]
-    moves += [(met_ref.at[0:3, inner], mt.at[0:3, inner]), (met_ref.at[6:9], mt.at[6:9])]
+    moves = [(code_ref, cd), (orient_ref, ori), (adj_ref, ad), (jac_ref, jc), (state_ref, st)]
+    moves += [(met_ref.at[rows], mt.at[rows]) for rows in (pl.ds(3, 3), pl.ds(0, 3), pl.ds(6, 3))]
     loads = [pltpu.make_async_copy(src, dst, load_sem.at[n]) for n, (src, dst) in enumerate(moves)]
     barrier = pltpu.get_barrier_semaphore()
     def signal(semaphore, target):
@@ -199,23 +192,6 @@
         @pl.when(greets[side])
         def _(side=side):
             signal(barrier, {**ids[side], "gz": jnp.where(tied[side], 0, 1) if side < 2 else 0})
-
-    for copy in loads:
-        copy.start()
-    for side in range(4):
-        @pl.when(jnp.logical_not(inner_side[side]))
-        def _(side=side):
-            blank = jnp.zeros((8, 128), f32)
-            if side < 2:
-                for ref, count in ((recv_u, 5), (recv_g, 3), (recv_w, 5)):
-                    for n in range(count):
-                        for half in range(2):
-                            ref[side, n, pl.ds(8 * half, 8)] = blank
-                if side == 0:
-                    recv_f[...] = jnp.zeros((8, 32), jnp.int32)
-            else:
-                for n in range(13):
-                    recv[place[side], n] = blank
 
     landing = [1, 0, 3, 2, 4]
     ends = [pl.ds(0, 16), pl.ds(112, 16)]
@@ -274,6 +250,23 @@
             def _(side=side):
                 answer(side, 1)
                 start_raw(side)
+
+    for copy in loads:
+        copy.start()
+    for side in range(4):
+        @pl.when(jnp.logical_not(inner_side[side]))
+        def _(side=side):
+            blank = jnp.zeros((8, 128), f32)
+            if side < 2:
+                for ref, count in ((recv_u, 5), (recv_g, 3), (recv_w, 5)):
+                    for n in range(count):
+                        for half in range(2):
+                            ref[side, n, pl.ds(8 * half, 8)] = blank
+                if side == 0:
+                    recv_f[...] = jnp.zeros((8, 32), jnp.int32)
+            else:
+                for n in range(13):
+                    recv[place[side], n] = blank
 
     def meet():
         pl.semaphore_wait(barrier, 2 * count(slow, greeted[2], greeted[3]) + 1)
@@ -373,7 +366,7 @@
                 nb[n, rows] = value
         return values
 
-    for load in loads[2:10]:
+    for load in loads[2:5]:
         load.wait()
 
     def pack(slot, values, flag=None, flip=None):
@@ -390,8 +383,7 @@
     for side in (1, 0):
         pl.when(early[side] & prompt)(weight_copies[side].start)
 
-    for load in loads[10:14]:
-        load.wait()
+    loads[5].wait()
     for slot, y, flag in ((0, 0, None), (1, 15, flag_y_top)):
         rows = pl.ds(y, 8, stride=16)
         values = convert(rows, keep=False)
@@ -408,7 +400,7 @@
         rows = pl.ds(y, 8, stride=16)
         return [nb[n, rows] for n in range(14)] + [mt[3 + n, rows] for n in range(3)]
 
-    loads[14].wait()
+    loads[6].wait()
 
     def load_x(rows):
         return [nb[n, rows] for n in range(14)] + [mt[n, rows] for n in range(3)]
@@ -454,9 +446,10 @@
         start_raw(1)
         weight_copies[1].start()
 
+    answered(2, here == 3)
     answered(0, here == 3)
 
-    loads[15].wait()
+    loads[7].wait()
     for n in range(5):
         tb[n, 0:128] = jnp.transpose(nb[n])
         tb[9 + n, 0:128] = jnp.transpose(nb[9 + n])
@@ -504,7 +497,7 @@
         add(acc, pl.ds(4 * ey + 4, 8, stride=16), to_u)
 
     answered(3, here == 2)
-    answered(2, iy >= 0)
+    answered(2, here != 3)
     answered(1, here == 0)
 
     def rows_z(chunk, a):
@@ -609,7 +602,7 @@
         finish(rows, [acc[n, rows] for n in range(5)])
 
     def x_rows_of(side, half):
-        return pl.ds(side * 112 + half * 8, 8)
+        return pl.ds(pl.multiple_of(side * 112 + half * 8, 8), 8)
 
     def x_flags(side, half):
         return mb[2 * side + half, 3] > 0.5
@@ -624,20 +617,33 @@
             jnp.broadcast_to(below_flags[5 + 2 * half : 6 + 2 * half], (8, 128)),
         )
 
-    for side in (1, 0):
-        for copy in raw_copies[landing[side]][-2:]:
-            on_side(side, copy.wait_recv)
+    def arrive(side, *waits):
+        for n in range(2):
+            @pl.when((side == n) & inner_side[n])
+            def _(n=n):
+                for wait in waits:
+                    wait(n)
+
+    @pl.loop(0, 2)
+    def _(turn):
+        side = jnp.where(here == 0, 1 - turn, turn)
+        arrive(
+            side,
+            lambda n: raw_copies[landing[n]][-2].wait_recv(),
+            lambda n: raw_copies[landing[n]][-1].wait_recv(),
+        )
         for half in range(2):
-            rows, flag = pl.ds(8 * half, 8), x_flags(side, half)
+            slot, rows, flag = 2 * side + half, pl.ds(8 * half, 8), x_flags(side, half)
             u = flipped([recv_u[side, n, rows] for n in range(5)], flag, flip_sub)
             normal = flipped([recv_g[side, n, rows] for n in range(3)], flag, flip_sub)
-            prim = primitives(u)
-            other, normal = outer_node(2 * side + half, load_x(x_rows_of(side, half)), prim, normal)
+            other, normal = outer_node(slot, load_x(x_rows_of(side, half)), primitives(u), normal)
             for n, value in enumerate([*other, *normal]):
-                xo[2 * side + half, n] = value
-
-    for side in (1, 0):
-        on_side(side, weight_copies[landing[side]].wait_recv)
+                xo[slot, n] = value
+
+    @pl.loop(0, 2)
+    def _(turn):
+        side = jnp.where(here == 0, 1 - turn, turn)
+        arrive(side, lambda n: weight_copies[landing[n]].wait_recv())
         for half in range(2):
             slot, rows = 2 * side + half, x_rows_of(side, half)
             w = flipped([recv_w[side, n, pl.ds(8 * half, 8)] for n in range(5)], x_flags(side, half), flip_sub)
@@ -688,7 +694,7 @@
                 vmem((2, 5, 16, 128), f32),
                 vmem((8, 32), jnp.int32),
                 vmem((4, 12, 8, 128), f32),
-                pltpu.SemaphoreType.DMA((16,)),
+                pltpu.SemaphoreType.DMA((8,)),
                 pltpu.SemaphoreType.DMA((3,)),
                 pltpu.SemaphoreType.DMA((3,)),
                 pltpu.SemaphoreType.DMA((8,)),

time: 12.9 us -> 12.7 us (0.984)
  the two profiles are of different devices: /device:TPU:160 before, /device:TPU:30 now
where the time goes in v7:
time: 12.7 us; the launch traced here: 12.6 us
  Pallas kernels  11.9 us (94%)
  local copies, waits for them, and re-layouts  0.73 us (6%)
    pallas_call x1, Pallas kernels, body(): pl.pallas_call(lambda *refs: kernel(nx, ny, *refs), out_shape=jax.ShapeDt...  11.9 us
    unnamed x1, local copies, waits for them, and re-layouts  0.73 us

profile of v7, /device:TPU:30, one launch (start us, length us, event | category | flops | bytes accessed | tf_op | source)
XLA Modules:
  0.0 12.6 jit_solution(17986185685884996735)
XLA Ops:
  0.0 11.9 %adjoint_residual.1 = f32[5,128,128]{2,1,0:T(8,128)S(1)} custom-call(f32[5,128,128]{2,1,0:T(8,128)} %bitcast.9, f32[5,128,128]{2,1,0:T(8,128)} %bitcast.10, f32[9,128,128]{2,1,0:T(8,128)} %bitcast.8, f32[128,128]{1,0:T(8,128)} %bitcast.11, s32[8,32]{1,0:T(8,128)} %bitcast.13, s32[24,32]{1,0:T(8,128)} %bitcast.12), custom_call_target="tpu_custom_call" | custom-call | tf_op jit(solution)/shard_map/adjoint_residual/pallas_call | solution.py:670
  11.9 0.7 %copy.8 = f32[5,8,16,128]{3,2,1,0:T(8,128)} copy(f32[5,8,16,128]{3,2,1,0:T(8,128)S(1)} %bitcast.7) | data formatting | bytes 655360

commit v8 on v7

--- a/solution.py
+++ b/solution.py
@@ -274,6 +274,7 @@
             @pl.when(early[side])
             def _(side=side):
                 answer(side, 0)
+                pl.when(jnp.logical_not(slow))(lambda: start_raw(side))
 
         signal(ready_sem.at[4], {"gz": 1})
         for side in (1, 2, 3):
@@ -285,8 +286,6 @@
     @pl.when((iz == 0) & jnp.logical_not(slow))
     def _():
         meet()
-        for side in (1, 0):
-            pl.when(early[side])(lambda side=side: start_raw(side))
 
     sub = lax.broadcasted_iota(jnp.int32, (8, 128), 0)
     lane = lax.broadcasted_iota(jnp.int32, (8, 128), 1)

time: 12.7 us -> 12.7 us (level)
  no operation moved by 1% of the time
where the time goes in v8:
time: 12.7 us; the launch traced here: 12.6 us
  Pallas kernels  11.9 us (94%)
  local copies, waits for them, and re-layouts  0.73 us (6%)
    pallas_call x1, Pallas kernels, body(): pl.pallas_call(lambda *refs: kernel(nx, ny, *refs), out_shape=jax.ShapeDt...  11.9 us
    unnamed x1, local copies, waits for them, and re-layouts  0.73 us

profile of v8, /device:TPU:30, one launch (start us, length us, event | category | flops | bytes accessed | tf_op | source)
XLA Modules:
  0.0 12.6 jit_solution(13149568503643050948)
XLA Ops:
  0.0 11.9 %adjoint_residual.1 = f32[5,128,128]{2,1,0:T(8,128)S(1)} custom-call(f32[5,128,128]{2,1,0:T(8,128)} %bitcast.9, f32[5,128,128]{2,1,0:T(8,128)} %bitcast.10, f32[9,128,128]{2,1,0:T(8,128)} %bitcast.8, f32[128,128]{1,0:T(8,128)} %bitcast.11, s32[8,32]{1,0:T(8,128)} %bitcast.13, s32[24,32]{1,0:T(8,128)} %bitcast.12), custom_call_target="tpu_custom_call" | custom-call | tf_op jit(solution)/shard_map/adjoint_residual/pallas_call | solution.py:669
  11.9 0.7 %copy.8 = f32[5,8,16,128]{3,2,1,0:T(8,128)} copy(f32[5,8,16,128]{3,2,1,0:T(8,128)S(1)} %bitcast.7) | data formatting | bytes 655360
